TPU v7x, 512 devices: a whole 4x8x8 slice. The times are simulated.
512 devices in a mesh: uly: 32 (over y, z_hi, core), blk: 16 (over z_lo, x).
Axes of the slice: x: 4, y: 8, z: 8 (z_hi: 2, z_lo: 4; z = z_hi * 4 + z_lo), core: 2. Of those that a mesh axis runs over, the one named last changes fastest.
Arguments:
- queries: bfloat16 [65536, 32, 128], P(('blk', 'uly')), may hold values from -6 to 6
- keys: bfloat16 [65536, 8, 128], P(('blk', 'uly')), may hold values from -6 to 6
- values: bfloat16 [65536, 8, 128], P(('blk', 'uly')), may hold values from -6 to 6
- grad_out: bfloat16 [65536, 32, 128], P(('blk', 'uly')), may hold values from -6 to 6
- lse: float32 [32, 65536], P('uly'), may hold values from 4 to 6
- delta: float32 [32, 65536], P('uly'), may hold values from -18 to 18
- block_keys: int32 [512, 5], replicated, may hold values from -1 to 511, as said below
Outputs:
- grad_queries: bfloat16 [65536, 32, 128], P(('blk', 'uly'))
- grad_keys: bfloat16 [65536, 8, 128], P(('blk', 'uly'))
- grad_values: bfloat16 [65536, 8, 128], P(('blk', 'uly'))
Inputs may be any that keep to these rules, and one draw needn't show every extreme that they name: `block_keys`: query block b lists itself first, then 5 - 1 distinct earlier blocks c with c >= 32 * (b // 32 - 1); entries are -1 only where fewer earlier blocks exist, after the listed ones.
All inputs are finite; a program needn't handle non-finite values.
Results may differ from a plain program's by a relative error of at most 0.0053.
Values may be sent and summed in bfloat16 or wider, within the bound.
A program may use at most 128 MiB of HBM per device.

v0:
```python
import math

import jax
import jax.numpy as jnp
from jax import lax
from jax.sharding import PartitionSpec as P

BLOCK = 128


def passed_along(block, axis, distance):
    devices = range(lax.axis_size(axis))
    route = [(i - distance, i) for i in devices if i - distance in devices]
    return lax.ppermute(block, axis, route)


def block_grads(
    query_rows,
    dout_rows,
    lse_rows,
    delta_rows,
    key_blocks,
    value_blocks,
    block_index,
    block_valid,
    block_diag,
    per_step,
):
    query_blocks = block_index.shape[0]
    width = key_blocks.shape[1]
    head_dim = key_blocks.shape[2]
    head_count = query_rows.shape[1]
    select = block_index.shape[1]
    step_count = query_blocks // per_step
    score_scale = 1.0 / math.sqrt(head_dim)
    query_steps = query_rows.reshape(step_count, per_step, width, head_count, head_dim)
    dout_steps = dout_rows.reshape(step_count, per_step, width, head_count, head_dim)
    lse_steps = lse_rows.reshape(head_count, step_count, per_step, width).transpose(1, 2, 0, 3)
    delta_steps = delta_rows.reshape(head_count, step_count, per_step, width).transpose(1, 2, 0, 3)
    safe_index = jnp.where(block_valid, block_index, 0).reshape(step_count, per_step, select)
    valid_steps = block_valid.reshape(step_count, per_step, select)
    diag_steps = block_diag.reshape(step_count, per_step, select)
    positions = jnp.arange(width, dtype=jnp.int32)
    causal = positions[None, :] <= positions[:, None]

    def advance(carry, inputs):
        key_acc, value_acc = carry
        query_part, dout_part, lse_part, delta_part, index_part, valid_part, diag_part = inputs
        key_part = key_blocks[index_part]
        value_part = value_blocks[index_part]
        scores = (
            jnp.einsum("pthd,pjsd->phtjs", query_part, key_part, preferred_element_type=jnp.float32)
            * score_scale
        )
        allowed = valid_part[:, None, None, :, None] & (
            jnp.logical_not(diag_part)[:, None, None, :, None] | causal[None, None, :, None, :]
        )
        probs = jnp.where(allowed, jnp.exp(scores - lse_part[:, :, :, None, None]), 0.0)
        dprobs = jnp.einsum(
            "pthd,pjsd->phtjs", dout_part, value_part, preferred_element_type=jnp.float32
        )
        dscores = probs * (dprobs - delta_part[:, :, :, None, None])
        probs_low = probs.astype(jnp.bfloat16)
        dscores_low = dscores.astype(jnp.bfloat16)
        grad_query = (
            jnp.einsum(
                "phtjs,pjsd->pthd", dscores_low, key_part, preferred_element_type=jnp.float32
            )
            * score_scale
        )
        grad_value = jnp.einsum(
            "phtjs,pthd->pjsd", probs_low, dout_part, preferred_element_type=jnp.float32
        )
        grad_key = (
            jnp.einsum(
                "phtjs,pthd->pjsd", dscores_low, query_part, preferred_element_type=jnp.float32
            )
            * score_scale
        )
        flat_index = index_part.reshape(-1)
        key_acc = key_acc.at[flat_index].add(grad_key.reshape(-1, width, head_dim))
        value_acc = value_acc.at[flat_index].add(grad_value.reshape(-1, width, head_dim))
        return ((key_acc, value_acc), grad_query)

    start = jnp.zeros((key_blocks.shape[0], width, head_dim), jnp.float32)
    (key_acc, value_acc), grad_query = lax.scan(
        advance,
        (start, start),
        (query_steps, dout_steps, lse_steps, delta_steps, safe_index, valid_steps, diag_steps),
    )
    return (grad_query.reshape(query_blocks * width, head_count, head_dim), key_acc, value_acc)


def shards(queries, keys, values, grad_out, lse, delta, block_keys):
    uly_count = lax.axis_size("uly")
    tokens_here, head_total, head_dim = queries.shape
    kv_heads = keys.shape[1]
    fold_count = uly_count // kv_heads
    slab_len = tokens_here * uly_count
    slab_blocks = slab_len // BLOCK
    per_step = math.gcd(slab_blocks, max(1, 512 // BLOCK))
    slab_index = lax.axis_index("blk")
    query_slab, dout_slab = (
        lax.all_to_all(queries, "uly", split_axis=1, concat_axis=0, tiled=True),
        lax.all_to_all(grad_out, "uly", split_axis=1, concat_axis=0, tiled=True),
    )
    repeat_count = head_total // kv_heads
    key_wide = jnp.repeat(keys, repeat_count, axis=1)
    value_wide = jnp.repeat(values, repeat_count, axis=1)
    key_here, value_here = (
        lax.all_to_all(key_wide, "uly", split_axis=1, concat_axis=0, tiled=True),
        lax.all_to_all(value_wide, "uly", split_axis=1, concat_axis=0, tiled=True),
    )
    key_slab = key_here[:, 0, :]
    value_slab = value_here[:, 0, :]
    lse_slab = lax.dynamic_slice_in_dim(lse, slab_index * slab_len, slab_len, 1)
    delta_slab = lax.dynamic_slice_in_dim(delta, slab_index * slab_len, slab_len, 1)
    slab_keys = lax.dynamic_slice_in_dim(block_keys, slab_index * slab_blocks, slab_blocks, 0)
    query_ids = slab_index * slab_blocks + jnp.arange(slab_blocks, dtype=jnp.int32)
    key_prev, value_prev = passed_along((key_slab, value_slab), "blk", 1)
    key_blocks = jnp.concatenate([key_prev, key_slab], 0).reshape(2 * slab_blocks, BLOCK, head_dim)
    value_blocks = jnp.concatenate([value_prev, value_slab], 0).reshape(
        2 * slab_blocks, BLOCK, head_dim
    )
    local_index = slab_keys - (slab_index - 1) * slab_blocks
    grad_query, key_acc, value_acc = block_grads(
        query_slab,
        dout_slab,
        lse_slab,
        delta_slab,
        key_blocks,
        value_blocks,
        local_index,
        slab_keys >= 0,
        slab_keys == query_ids[:, None],
        per_step,
    )
    key_back, value_back = passed_along((key_acc[:slab_blocks], value_acc[:slab_blocks]), "blk", -1)
    key_total = (key_acc[slab_blocks:] + key_back).reshape(slab_len, head_dim)
    value_total = (value_acc[slab_blocks:] + value_back).reshape(slab_len, head_dim)
    key_back, value_back = (
        lax.all_to_all(
            key_total.reshape(uly_count, tokens_here, head_dim),
            "uly",
            split_axis=0,
            concat_axis=1,
            tiled=True,
        ),
        lax.all_to_all(
            value_total.reshape(uly_count, tokens_here, head_dim),
            "uly",
            split_axis=0,
            concat_axis=1,
            tiled=True,
        ),
    )
    grad_keys = (
        key_back.reshape(kv_heads, fold_count, tokens_here, head_dim).sum(1).transpose(1, 0, 2)
    )
    grad_values = (
        value_back.reshape(kv_heads, fold_count, tokens_here, head_dim).sum(1).transpose(1, 0, 2)
    )
    grad_queries = lax.all_to_all(
        grad_query.astype(jnp.bfloat16), "uly", split_axis=0, concat_axis=1, tiled=True
    )
    return (grad_queries, grad_keys.astype(jnp.bfloat16), grad_values.astype(jnp.bfloat16))


def solution(mesh):
    return jax.shard_map(
        shards,
        mesh=mesh,
        in_specs=(
            P(("blk", "uly"), None, None),
            P(("blk", "uly"), None, None),
            P(("blk", "uly"), None, None),
            P(("blk", "uly"), None, None),
            P("uly", None),
            P("uly", None),
            P(),
        ),
        out_specs=(
            P(("blk", "uly"), None, None),
            P(("blk", "uly"), None, None),
            P(("blk", "uly"), None, None),
        ),
        check_vma=False,
    )
```

profile of v0, /device:TPU:6, one launch (start us, length us, event | category | flops | bytes accessed | tf_op | source)
XLA Modules:
  0.0 633.7 jit_solution(202664600943508312)
XLA Ops:
  2.9 15.9 %all-to-all-start.2 = ((bf16[128,32,128]{2,0,1:T(8,128)(2,1)}), bf16[128,32,128]{2,0,1:T(8,128)(2,1)S(1)}, u32[]{:S(2)}, u32[]{:S(2)}) async-start(bf16[128,32,128]{2,0,1:T(8,128)(2,1)} %bitcast.13), calls=%async_computation.2 | async-start | bytes 2097152 | tf_op jit(solution)/shard_map/all_to_all | solution.py:112
  18.9 31.1 %all-to-all-done.2 = bf16[128,32,128]{2,0,1:T(8,128)(2,1)S(1)} async-done(((bf16[128,32,128]{2,0,1:T(8,128)(2,1)}), bf16[128,32,128]{2,0,1:T(8,128)(2,1)S(1)}, u32[]{:S(2)}, u32[]{:S(2)}) %all-to-all-start.2) | async-done | bytes 1048608 | tf_op jit(solution)/shard_map/all_to_all | solution.py:112
  51.3 6.1 all-to-all-start
  58.8 29.4 %all-to-all-done = bf16[128,32,128]{2,0,1:T(8,128)(2,1)S(1)} async-done(((bf16[128,32,128]{2,0,1:T(8,128)(2,1)}), bf16[128,32,128]{2,0,1:T(8,128)(2,1)S(1)}, u32[]{:S(2)}, u32[]{:S(2)}) %all-to-all-start) | async-done | bytes 1048608 | tf_op jit(solution)/shard_map/all_to_all | solution.py:111
  88.2 6.5 %all-to-all-start.1 = ((bf16[128,32,128]{2,0,1:T(8,128)(2,1)}), bf16[128,32,128]{2,0,1:T(8,128)(2,1)}, u32[]{:S(2)}, u32[]{:S(2)}) async-start(bf16[128,32,128]{2,0,1:T(8,128)(2,1)} %copy.36), calls=%async_computation.1 | async-start | bytes 2097152 | tf_op jit(solution)/shard_map/all_to_all | solution.py:104
  98.7 26.3 %all-to-all-done.1 = bf16[128,32,128]{2,0,1:T(8,128)(2,1)} async-done(((bf16[128,32,128]{2,0,1:T(8,128)(2,1)}), bf16[128,32,128]{2,0,1:T(8,128)(2,1)}, u32[]{:S(2)}, u32[]{:S(2)}) %all-to-all-start.1) | async-done | bytes 1048608 | tf_op jit(solution)/shard_map/all_to_all | solution.py:104
  125.1 6.9 %all-to-all-start.3 = ((bf16[128,32,128]{2,0,1:T(8,128)(2,1)}), bf16[128,32,128]{2,0,1:T(8,128)(2,1)}, u32[]{:S(2)}, u32[]{:S(2)}) async-start(bf16[128,32,128]{2,0,1:T(8,128)(2,1)} %copy.38), calls=%async_computation.3 | async-start | bytes 2097152 | tf_op jit(solution)/shard_map/all_to_all | solution.py:105
  134.4 25.9 %collective-permute-done.1 = bf16[4096,128]{1,0:T(8,128)(2,1)} collective-permute-done((bf16[4096,128]{1,0:T(8,128)(2,1)S(1)}, bf16[4096,128]{1,0:T(8,128)(2,1)}, u32[]{:S(2)}, u32[]{:S(2)}) %collective-permute-start.1) | collective-permute-done | bytes 1048608 | tf_op jit(solution)/shard_map/ppermute | solution.py:14
  163.0 22.3 %collective-permute-done = bf16[4096,128]{1,0:T(8,128)(2,1)S(1)} collective-permute-done((bf16[4096,128]{1,0:T(8,128)(2,1)S(1)}, bf16[4096,128]{1,0:T(8,128)(2,1)S(1)}, u32[]{:S(2)}, u32[]{:S(2)}) %collective-permute-start) | collective-permute-done | bytes 1048608 | tf_op jit(solution)/shard_map/ppermute | solution.py:14
  191.7 185.7 %while.15 = (s32[]{:T(128)}, f32[64,128,128]{2,1,0:T(8,128)}, f32[64,128,128]{2,1,0:T(8,128)}, bf16[8,4,128,1,128]{4,2,1,0,3:T(8,128)(2,1)}, s32[8,4,5]{2,1,0:T(...) while((s32[]{:T(128)}, f32[64,128,128]{2,1,0:T(8,128)}, ...), condition=%wide.region_3.4_spmd.clone, body=%wide.region_0.3_spmd.clone.sunk | while | flops 423511168 | bytes 27447200 | solution.py:86
  200.6 6.0 scatter_fusion
  207.8 6.0 scatter_fusion.1
  223.8 6.0 scatter_fusion
  231.1 6.0 scatter_fusion.1
  247.1 5.9 scatter_fusion
  254.2 5.9 scatter_fusion.1
  270.2 6.0 scatter_fusion
  277.4 6.0 scatter_fusion.1
  293.4 6.0 scatter_fusion
  300.6 6.0 scatter_fusion.1
  316.7 6.0 scatter_fusion
  323.9 6.0 scatter_fusion.1
  339.9 5.9 scatter_fusion
  347.0 5.9 scatter_fusion.1
  363.1 6.0 scatter_fusion
  370.2 6.0 scatter_fusion.1
  385.7 10.8 %all-to-all-start.4 = ((bf16[32,2,8192]{2,1,0:T(2,128)(2,1)}), bf16[32,2,8192]{2,1,0:T(2,128)(2,1)S(1)}, u32[]{:S(2)}, u32[]{:S(2)}) async-start(bf16[32,2,8192]{2,1,0:T(2,128)(2,1)} %reshape.259), calls=%async_computation.4 | async-start | bytes 2097152 | tf_op jit(solution)/shard_map/all_to_all | solution.py:163
  396.5 57.5 %collective-permute-done.3 = f32[32,128,128]{2,1,0:T(8,128)} collective-permute-done((f32[32,128,128]{2,1,0:T(8,128)}, f32[32,128,128]{2,1,0:T(8,128)}, u32[]{:S(2)}, u32[]{:S(2)}) %collective-permute-start.3) | collective-permute-done | bytes 2097184 | tf_op jit(solution)/shard_map/ppermute | solution.py:14
  458.0 10.2 %all-to-all-start.6 = ((f32[32,128,128]{2,1,0:T(8,128)}), f32[32,128,128]{2,1,0:T(8,128)S(1)}, u32[]{:S(2)}, u32[]{:S(2)}) async-start(f32[32,128,128]{2,1,0:T(8,128)} %slice_add_fusion), calls=%async_computation.6 | async-start | bytes 4194304 | tf_op jit(solution)/shard_map/all_to_all | solution.py:149
  472.1 89.2 %collective-permute-done.2 = f32[32,128,128]{2,1,0:T(8,128)S(1)} collective-permute-done((f32[32,128,128]{2,1,0:T(8,128)S(1)}, f32[32,128,128]{2,1,0:T(8,128)S(1)}, u32[]{:S(2)}, u32[]{:S(2)}) %collective-permute-start.2) | collective-permute-done | bytes 2097184 | tf_op jit(solution)/shard_map/ppermute | solution.py:14
  564.3 11.8 %all-to-all-start.5 = ((f32[32,128,128]{2,1,0:T(8,128)}), f32[32,128,128]{2,1,0:T(8,128)}, u32[]{:S(2)}, u32[]{:S(2)}) async-start(f32[32,128,128]{2,1,0:T(8,128)} %slice_add_fusion.1), calls=%async_computation.5 | async-start | bytes 4194304 | tf_op jit(solution)/shard_map/all_to_all | solution.py:142
  579.9 51.1 %all-to-all-done.5 = f32[32,128,128]{2,1,0:T(8,128)} async-done(((f32[32,128,128]{2,1,0:T(8,128)}), f32[32,128,128]{2,1,0:T(8,128)}, u32[]{:S(2)}, u32[]{:S(2)}) %all-to-all-start.5) | async-done | bytes 2097184 | tf_op jit(solution)/shard_map/all_to_all | solution.py:142
  (223 shorter events, 135.6 us)
Async XLA Ops:
  0.6 18.2 %copy-start.8 = (bf16[128,8,128]{2,1,0:T(8,128)(2,1)S(1)}, bf16[128,8,128]{2,1,0:T(8,128)(2,1)}, u32[]{:S(2)}) copy-start(bf16[128,8,128]{2,1,0:T(8,128)(2,1)} %param.10) | copy-start | bytes 786436
  2.9 47.2 %all-to-all-start.2 = ((bf16[128,32,128]{2,0,1:T(8,128)(2,1)}), bf16[128,32,128]{2,0,1:T(8,128)(2,1)S(1)}, u32[]{:S(2)}, u32[]{:S(2)}) async-start(bf16[128,32,128]{2,0,1:T(8,128)(2,1)} %bitcast.13), calls=%async_computation.2 | async-start | bytes 2097152 | tf_op jit(solution)/shard_map/all_to_all | solution.py:112
  18.8 38.5 %copy-start.6 = (bf16[128,32,128]{2,1,0:T(8,128)(2,1)S(1)}, bf16[128,32,128]{2,1,0:T(8,128)(2,1)}, u32[]{:S(2)}) copy-start(bf16[128,32,128]{2,1,0:T(8,128)(2,1)} %param.9) | copy-start | bytes 3145732
  51.3 36.9 %all-to-all-start = ((bf16[128,32,128]{2,0,1:T(8,128)(2,1)}), bf16[128,32,128]{2,0,1:T(8,128)(2,1)S(1)}, u32[]{:S(2)}, u32[]{:S(2)}) async-start(bf16[128,32,128]{2,0,1:T(8,128)(2,1)} %bitcast.3), calls=%async_computation | async-start | bytes 2097152 | tf_op jit(solution)/shard_map/all_to_all | solution.py:111
  58.7 37.9 %copy-start.7 = (bf16[128,32,128]{2,1,0:T(8,128)(2,1)S(1)}, bf16[128,32,128]{2,1,0:T(8,128)(2,1)}, u32[]{:S(2)}) copy-start(bf16[128,32,128]{2,1,0:T(8,128)(2,1)} %param.12) | copy-start | bytes 3145732
  88.2 36.9 %all-to-all-start.1 = ((bf16[128,32,128]{2,0,1:T(8,128)(2,1)}), bf16[128,32,128]{2,0,1:T(8,128)(2,1)}, u32[]{:S(2)}, u32[]{:S(2)}) async-start(bf16[128,32,128]{2,0,1:T(8,128)(2,1)} %copy.36), calls=%async_computation.1 | async-start | bytes 2097152 | tf_op jit(solution)/shard_map/all_to_all | solution.py:104
  94.7 65.6 %collective-permute-start.1 = (bf16[4096,128]{1,0:T(8,128)(2,1)S(1)}, bf16[4096,128]{1,0:T(8,128)(2,1)}, u32[]{:S(2)}, u32[]{:S(2)}) collective-permute-start(bf16[4096,128]{1,0:T(8,128)(2,1)S(1)} %bitcast.199), channel_id=1, source_target_pairs={{0,1},{1,2},{2,3},{3,4},{4,5},{5,6},{6,7},{7,8},{8,9},{9,10},{10,1... | collective-permute-start | bytes 3145736 | tf_op jit(solution)/shard_map/ppermute | solution.py:14
  96.6 35.4 %copy-start.9 = (s32[512,5]{0,1:T(8,128)S(1)}, s32[512,5]{0,1:T(8,128)}, u32[]{:S(2)}) copy-start(s32[512,5]{0,1:T(8,128)} %param.15) | copy-start | bytes 30724
  125.1 61.7 %all-to-all-start.3 = ((bf16[128,32,128]{2,0,1:T(8,128)(2,1)}), bf16[128,32,128]{2,0,1:T(8,128)(2,1)}, u32[]{:S(2)}, u32[]{:S(2)}) async-start(bf16[128,32,128]{2,0,1:T(8,128)(2,1)} %copy.38), calls=%async_computation.3 | async-start | bytes 2097152 | tf_op jit(solution)/shard_map/all_to_all | solution.py:105
  132.2 53.1 %collective-permute-start = (bf16[4096,128]{1,0:T(8,128)(2,1)S(1)}, bf16[4096,128]{1,0:T(8,128)(2,1)S(1)}, u32[]{:S(2)}, u32[]{:S(2)}) collective-permute-start(bf16[4096,128]{1,0:T(8,128)(2,1)S(1)} %bitcast.201), channel_id=1, source_target_pairs={{0,1},{1,2},{2,3},{3,4},{4,5},{5,6},{6,7},{7,8},{8,9},{9,10},{10,1... | collective-permute-start | bytes 3145736 | tf_op jit(solution)/shard_map/ppermute | solution.py:14
  194.1 3.9 copy-start
  207.8 6.0 copy-start.1
  217.3 3.9 copy-start
  231.0 6.0 copy-start.1
  240.6 3.9 copy-start
  254.2 5.9 copy-start.1
  277.4 6.0 copy-start.1
  287.0 3.9 copy-start
  300.6 6.0 copy-start.1
  310.2 3.9 copy-start
  323.9 6.0 copy-start.1
  333.5 3.9 copy-start
  347.0 5.9 copy-start.1
  356.6 3.9 copy-start
  370.2 6.0 copy-start.1
  377.4 5.7 copy-start.5
  380.7 73.4 %collective-permute-start.3 = (f32[32,128,128]{2,1,0:T(8,128)}, f32[32,128,128]{2,1,0:T(8,128)}, u32[]{:S(2)}, u32[]{:S(2)}) collective-permute-start(f32[32,128,128]{2,1,0:T(8,128)} %slice.15), channel_id=1, source_target_pairs={{1,0},{2,1},{3,2},{4,3},{5,4},{6,5},{7,6},{8,7},{9,8},{10,9},{11,1... | collective-permute-start | bytes 6291464 | tf_op jit(solution)/shard_map/ppermute | solution.py:14
  385.7 72.3 %all-to-all-start.4 = ((bf16[32,2,8192]{2,1,0:T(2,128)(2,1)}), bf16[32,2,8192]{2,1,0:T(2,128)(2,1)S(1)}, u32[]{:S(2)}, u32[]{:S(2)}) async-start(bf16[32,2,8192]{2,1,0:T(2,128)(2,1)} %reshape.259), calls=%async_computation.4 | async-start | bytes 2097152 | tf_op jit(solution)/shard_map/all_to_all | solution.py:163
  458.0 104.8 %all-to-all-start.6 = ((f32[32,128,128]{2,1,0:T(8,128)}), f32[32,128,128]{2,1,0:T(8,128)S(1)}, u32[]{:S(2)}, u32[]{:S(2)}) async-start(f32[32,128,128]{2,1,0:T(8,128)} %slice_add_fusion), calls=%async_computation.6 | async-start | bytes 4194304 | tf_op jit(solution)/shard_map/all_to_all | solution.py:149
  468.3 93.0 %copy-start.2 = (f32[64,128,128]{2,1,0:T(8,128)S(1)}, f32[64,128,128]{2,1,0:T(8,128)}, u32[]{:S(2)}) copy-start(f32[64,128,128]{2,1,0:T(8,128)} %get-tuple-element.78) | copy-start | bytes 12582916
  470.2 91.1 %collective-permute-start.2 = (f32[32,128,128]{2,1,0:T(8,128)S(1)}, f32[32,128,128]{2,1,0:T(8,128)S(1)}, u32[]{:S(2)}, u32[]{:S(2)}) collective-permute-start(f32[32,128,128]{2,1,0:T(8,128)S(1)} %slice.13), channel_id=1, source_target_pairs={{1,0},{2,1},{3,2},{4,3},{5,4},{6,5},{7,6},{8,7},{9,8},{10,9},{11,1... | collective-permute-start | bytes 6291464 | tf_op jit(solution)/shard_map/ppermute | solution.py:14
  564.3 66.8 %all-to-all-start.5 = ((f32[32,128,128]{2,1,0:T(8,128)}), f32[32,128,128]{2,1,0:T(8,128)}, u32[]{:S(2)}, u32[]{:S(2)}) async-start(f32[32,128,128]{2,1,0:T(8,128)} %slice_add_fusion.1), calls=%async_computation.5 | async-start | bytes 4194304 | tf_op jit(solution)/shard_map/all_to_all | solution.py:142
  (3 other events, 7.1 us)
where the time goes:
time: 639 us; the launch traced here: 634 us
  waiting for transfers between devices  333 us (52%)
  other arithmetic  109 us (17%)
  starting transfers between devices  75.9 us (12%)
  local copies, waits for them, and re-layouts  69.2 us (11%)
  matrix products  45.1 us (7%)
    ppermute x4, waiting for transfers between devices, passed_along(): return lax.ppermute(block, axis, route)  195 us
    all_to_all x1, waiting for transfers between devices, shards(): lax.all_to_all(key_total.reshape(uly_count, tokens_here, head_dim), 'uly'...  51.1 us
    scatter-add x8, other arithmetic, advance(): value_acc.at[flat_index].add(grad_value.reshape(-1, width, head_dim))  47.7 us
    scatter-add x8, other arithmetic, advance(): key_acc = key_acc.at[flat_index].add(grad_key.reshape(-1, width, head_dim))  47.6 us
    all_to_all x1, waiting for transfers between devices, shards(): lax.all_to_all(value_wide, 'uly', split_axis=1, concat_axis=0, tiled=True)  31.1 us
    all_to_all x1, waiting for transfers between devices, shards(): lax.all_to_all(key_wide, 'uly', split_axis=1, concat_axis=0, tiled=True)  29.4 us
    all_to_all x1, waiting for transfers between devices, shards(): lax.all_to_all(queries, 'uly', split_axis=1, concat_axis=0, tiled=True)  26.3 us
    gather x8, local copies, waits for them, and re-layouts, advance(): value_part = value_blocks[index_part]  18.1 us
  transfers between devices with their start and end apart: 11, of which 8 were waited for; matrix products, arithmetic and copies ran while one was open for 4% of the time, Pallas kernels for 0%

commit v1 on v0

v1 whole, which is shorter than its diff:
```python
import functools
import math

import jax
import jax.numpy as jnp
from jax import lax
from jax.experimental import pallas as pl
from jax.experimental.pallas import tpu as pltpu
from jax.sharding import PartitionSpec as P

BLOCK = 128
OFF = -1e30


def grads_kernel(scale, idx, bias, lse, delta, q, do, keys, vals, dq, dk, dv):
    step = pl.program_id(0)
    select = idx.shape[1]
    rows = q.shape[1]
    heads = rows // BLOCK

    @pl.when(step == 0)
    def _():
        dk[...] = jnp.zeros_like(dk)
        dv[...] = jnp.zeros_like(dv)

    places = [idx[step, j] for j in range(select)]
    kcat = jnp.concatenate([keys[c] for c in places], 0)
    vcat = jnp.concatenate([vals[c] for c in places], 0)
    qb, dob = q[0], do[0]
    nt = (((1,), (1,)), ((), ()))
    nn = (((1,), (0,)), ((), ()))
    s = lax.dot_general(kcat, qb, nt, preferred_element_type=jnp.float32)
    dp = lax.dot_general(vcat, dob, nt, preferred_element_type=jnp.float32)
    lse_row, delta_row = lse[0], delta[0]
    probs, dscores = [], []
    for j in range(select):
        part = slice(j * BLOCK, (j + 1) * BLOCK)
        p = jnp.exp(s[part] * scale - (lse_row - bias[step, j]))
        if j == 0:
            key_at = lax.broadcasted_iota(jnp.int32, (BLOCK, rows), 0)
            query_at = lax.broadcasted_iota(jnp.int32, (BLOCK, rows), 1) // heads
            p = jnp.where(key_at <= query_at, p, 0.0)
        ds = p * (dp[part] - delta_row)
        probs.append(p.astype(jnp.bfloat16))
        dscores.append(ds.astype(jnp.bfloat16))
    pcat = jnp.concatenate(probs, 0)
    dscat = jnp.concatenate(dscores, 0)
    dv_part = lax.dot_general(pcat, dob, nn, preferred_element_type=jnp.float32)
    dk_part = lax.dot_general(dscat, qb, nn, preferred_element_type=jnp.float32)
    dqt = lax.dot_general(kcat.T, dscat, nn, preferred_element_type=jnp.float32)
    dq[0] = (dqt * scale).T.astype(jnp.bfloat16)
    for j, c in enumerate(places):
        part = slice(j * BLOCK, (j + 1) * BLOCK)
        dk[c] += dk_part[part] * scale
        dv[c] += dv_part[part]


def local_grads(idx, bias, lse, delta, q, do, keys, vals):
    steps, rows, hd = q.shape
    places = keys.shape[0]
    select = idx.shape[1]
    row = pl.BlockSpec((1, 1, rows), lambda i, *_: (i, 0, 0))
    tile = pl.BlockSpec((1, rows, hd), lambda i, *_: (i, 0, 0))
    whole = pl.BlockSpec(
        (places, BLOCK, hd), lambda i, *_: (0, 0, 0), pipeline_mode=pl.Buffered(1)
    )
    acc = jax.ShapeDtypeStruct((places, BLOCK, hd), jnp.float32)
    return pl.pallas_call(
        functools.partial(grads_kernel, 1.0 / math.sqrt(hd)),
        out_shape=(jax.ShapeDtypeStruct(q.shape, jnp.bfloat16), acc, acc),
        grid_spec=pltpu.PrefetchScalarGridSpec(
            num_scalar_prefetch=2,
            grid=(steps,),
            in_specs=[row, row, tile, tile, whole, whole],
            out_specs=(tile, whole, whole),
        ),
        compiler_params=pltpu.CompilerParams(vmem_limit_bytes=48 << 20),
        cost_estimate=pl.CostEstimate(
            flops=steps * 10 * rows * select * BLOCK * hd,
            bytes_accessed=4 * places * BLOCK * hd * 3,
            transcendentals=steps * rows * select * BLOCK,
        ),
        name="grads",
    )(idx, bias, lse, delta, q, do, keys, vals)


def shards(queries, keys, values, grad_out, lse, delta, block_keys):
    uly = lax.axis_size("uly")
    tokens, heads, hd = queries.shape
    kvh = keys.shape[1]
    group = heads // kvh
    fold = uly // kvh
    u, slab = lax.axis_index("uly"), lax.axis_index("blk")
    blks = lax.axis_size("blk")
    ys = [[y * fold + r for y in range(kvh)] for r in range(fold)]
    rs = [[y * fold + r for r in range(fold)] for y in range(kvh)]

    def over(x, groups):
        return lax.all_to_all(
            x, "uly", split_axis=0, concat_axis=0, axis_index_groups=groups, tiled=True
        )

    def by_group(x):
        return x.reshape(tokens, kvh, group, hd).transpose(1, 0, 2, 3)

    q = over(by_group(queries), ys).reshape(kvh, tokens * group, hd)
    do = over(by_group(grad_out), ys).reshape(kvh, tokens * group, hd)

    def gathered(x):
        quarter = over(x.transpose(1, 0, 2), ys)
        own = lax.all_gather(
            quarter, "uly", axis=0, axis_index_groups=rs, tiled=True
        )
        prev = lax.ppermute(own, "blk", [(i, i + 1) for i in range(blks - 1)])
        return jnp.concatenate([prev, own], 0)

    k_all, v_all = gathered(keys), gathered(values)

    slab_len = uly * tokens

    def rows_of(x):
        mine = lax.dynamic_slice_in_dim(x, slab * slab_len, slab_len, 1)
        mine = mine.reshape(kvh, fold, tokens).transpose(1, 0, 2)
        mine = over(mine, rs).reshape(group, kvh, tokens)
        return mine.transpose(1, 2, 0).reshape(kvh, 1, tokens * group)

    lse_rows, delta_rows = rows_of(lse), rows_of(delta)

    own_blocks = lax.dynamic_slice_in_dim(block_keys, slab * uly, uly, 0)
    own_blocks = lax.dynamic_index_in_dim(
        own_blocks.reshape(kvh, fold, -1), u % fold, 1, keepdims=False
    )
    own_at = jnp.where(own_blocks >= 0, own_blocks, own_blocks[:, :1])
    rel = own_at - (slab - 1) * uly
    part, home = rel // uly, rel % uly
    idx = part * uly + (home % fold) * kvh + home // fold
    bias = jnp.where(own_blocks >= 0, 0.0, OFF).astype(jnp.float32)

    dq, dk, dv = local_grads(idx, bias, lse_rows, delta_rows, q, do, k_all, v_all)

    grad_q = over(dq.reshape(kvh, tokens, group, hd), ys)
    grad_q = grad_q.transpose(1, 0, 2, 3).reshape(tokens, heads, hd)

    def sent_home(acc):
        back = lax.ppermute(
            acc[:uly].astype(jnp.bfloat16), "blk", [(i + 1, i) for i in range(blks - 1)]
        )
        total = (acc[uly:] + back).astype(jnp.bfloat16)
        parts = over(total, rs).reshape(fold, kvh, tokens, hd)
        summed = parts.astype(jnp.float32).sum(0).astype(jnp.bfloat16)
        return over(summed, ys).transpose(1, 0, 2)

    return grad_q, sent_home(dk), sent_home(dv)


def solution(mesh):
    data = P(("blk", "uly"), None, None)
    return jax.shard_map(
        shards,
        mesh=mesh,
        in_specs=(data, data, data, data, P("uly", None), P("uly", None), P()),
        out_specs=(data, data, data),
        check_vma=False,
    )
```

time: 639 us -> 349 us (0.55)
  waiting for transfers between devices: 333 us -> 220 us
  other arithmetic: 109 us -> 11.9 us
  local copies, waits for them, and re-layouts: 69.2 us -> 17.4 us
  matrix products: 45.1 us -> 0 us
  Pallas kernels: 0 us -> 14.3 us
  between operations: 0.86 us -> 14.3 us
  starting transfers between devices: 75.9 us -> 68.3 us
    scatter-add x16 -> x0, other arithmetic: 95.3 us -> none  [the longest x8 47.7 us: advance(): value_acc.at[flat_index].add(grad_value.reshape(-1, width, head_dim))]
    ppermute x4, waiting for transfers between devices: 195 us -> 108 us  [the longest x2 68.4 us: sent_home(): lax.ppermute(acc[:uly].astype(jnp.bfloat16), 'blk', [(i + 1, i) for i in...]
    dot_general x40 -> x0, matrix products: 45.1 us -> none  [the longest x8 12.4 us: advance(): jnp.einsum('pthd,pjsd->phtjs', query_part, key_part, preferred_element_ty...]
    gather x16 -> x0, local copies, waits for them, and re-layouts: 36.2 us -> none  [the longest x8 18.1 us: advance(): value_part = value_blocks[index_part]]
    all_to_all x7 -> x11, waiting for transfers between devices: 138 us -> 109 us  [over(): lax.all_to_all(x, 'uly', split_axis=0, concat_axis=0, axis_index_groups=g...]
    pallas_call x0 -> x1, Pallas kernels: none -> 14.3 us  [local_grads(): pl.pallas_call(functools.partial(grads_kernel, 1.0 / math.sqrt(hd)), out_...]
    all_to_all x7 -> x11, starting transfers between devices: 68.2 us -> 59.3 us  [over(): lax.all_to_all(x, 'uly', split_axis=0, concat_axis=0, axis_index_groups=g...]
    broadcast_in_dim x4 -> x0, local copies, waits for them, and re-layouts: 7.39 us -> none  [the longest x2 4.97 us: block_grads(): start = jnp.zeros((key_blocks.shape[0], width, head_dim), jnp.float32)]
  transfers between devices with their start and end apart: 11 -> 17, of which waited for: 8 -> 13; matrix products, arithmetic and copies ran while one was open for 4% -> 7% of each run, Pallas kernels for 0% -> 0%
where the time goes in v1:
time: 349 us; the launch traced here: 346 us
  waiting for transfers between devices  220 us (63%)
  starting transfers between devices  68.3 us (20%)
  local copies, waits for them, and re-layouts  17.4 us (5%)
  Pallas kernels  14.3 us (4%)
  between operations  14.3 us (4%)
  other arithmetic  11.9 us (3%)
    all_to_all x11, waiting for transfers between devices, over(): lax.all_to_all(x, 'uly', split_axis=0, concat_axis=0, axis_index_groups=g...  109 us
    ppermute x2, waiting for transfers between devices, sent_home(): lax.ppermute(acc[:uly].astype(jnp.bfloat16), 'blk', [(i + 1, i) for i in...  68.4 us
    all_to_all x11, starting transfers between devices, over(): lax.all_to_all(x, 'uly', split_axis=0, concat_axis=0, axis_index_groups=g...  59.3 us
    ppermute x2, waiting for transfers between devices, gathered(): prev = lax.ppermute(own, 'blk', [(i, i + 1) for i in range(blks - 1)])  40.1 us
    pallas_call x1, Pallas kernels, local_grads(): pl.pallas_call(functools.partial(grads_kernel, 1.0 / math.sqrt(hd)), out_...  14.3 us
  transfers between devices with their start and end apart: 17, of which 13 were waited for; matrix products, arithmetic and copies ran while one was open for 7% of the time, Pallas kernels for 0%

profile of v1, /device:TPU:6, one launch (start us, length us, event | category | flops | bytes accessed | tf_op | source)
XLA Modules:
  0.0 346.1 jit_solution(10456801640290821195)
XLA Ops:
  7.2 1.8 copy.45
  9.0 7.1 %all-to-all-start.5 = ((bf16[8,128,128]{2,1,0:T(8,128)(2,1)}), bf16[8,128,128]{2,1,0:T(8,128)(2,1)S(1)}, u32[]{:S(2)}, u32[]{:S(2)}) async-start(bf16[8,128,128]{2,1,0:T(8,128)(2,1)} %bitcast.36), calls=%async_computation.5 | async-start | bytes 524288 | tf_op jit(solution)/shard_map/all_to_all | solution.py:99
  16.1 11.8 %all-to-all-done.5 = bf16[8,128,128]{2,1,0:T(8,128)(2,1)S(1)} async-done(((bf16[8,128,128]{2,1,0:T(8,128)(2,1)}), bf16[8,128,128]{2,1,0:T(8,128)(2,1)S(1)}, u32[]{:S(2)}, u32[]{:S(2)}) %all-to-all-start.5) | async-done | bytes 262176 | tf_op jit(solution)/shard_map/all_to_all | solution.py:99
  30.0 10.3 %all-to-all-start = ((f32[4,8,128]{2,1,0:T(8,128)}), f32[4,8,128]{2,1,0:T(8,128)S(1)}, u32[]{:S(2)}, u32[]{:S(2)}) async-start(f32[4,8,128]{2,1,0:T(8,128)} %copy.26), calls=%async_computation | async-start | bytes 32768 | tf_op jit(solution)/shard_map/all_to_all | solution.py:99
  40.9 7.2 %all-to-all-done = f32[4,8,128]{2,1,0:T(8,128)S(1)} async-done(((f32[4,8,128]{2,1,0:T(8,128)}), f32[4,8,128]{2,1,0:T(8,128)S(1)}, u32[]{:S(2)}, u32[]{:S(2)}) %all-to-all-start) | async-done | bytes 16416 | tf_op jit(solution)/shard_map/all_to_all | solution.py:99
  48.1 3.3 all-to-all-start.1
  53.0 8.4 %all-to-all-done.1 = f32[4,8,128]{2,1,0:T(8,128)S(1)} async-done(((f32[4,8,128]{2,1,0:T(8,128)}), f32[4,8,128]{2,1,0:T(8,128)S(1)}, u32[]{:S(2)}, u32[]{:S(2)}) %all-to-all-start.1) | async-done | bytes 16416 | tf_op jit(solution)/shard_map/all_to_all | solution.py:99
  61.4 3.4 all-to-all-start.4
  66.2 11.0 %all-to-all-done.4 = bf16[8,128,128]{2,1,0:T(8,128)(2,1)S(1)} async-done(((bf16[8,128,128]{2,1,0:T(8,128)(2,1)}), bf16[8,128,128]{2,1,0:T(8,128)(2,1)S(1)}, u32[]{:S(2)}, u32[]{:S(2)}) %all-to-all-start.4) | async-done | bytes 262176 | tf_op jit(solution)/shard_map/all_to_all | solution.py:99
  77.2 3.6 %all-to-all-start.2 = ((bf16[8,128,4,128]{3,2,1,0:T(4,128)(2,1)}), bf16[8,128,4,128]{3,2,1,0:T(4,128)(2,1)S(1)}, u32[]{:S(2)}, u32[]{:S(2)}) async-start(bf16[8,128,4,128]{3,2,1,0:T(4,128)(2,1)} %bitcast.35), calls=%async_computation.2 | async-start | bytes 2097152 | tf_op jit(solution)/shard_map/all_to_all | solution.py:99
  82.9 27.0 %all-to-all-done.2 = bf16[8,128,4,128]{3,2,1,0:T(4,128)(2,1)S(1)} async-done(((bf16[8,128,4,128]{3,2,1,0:T(4,128)(2,1)}), bf16[8,128,4,128]{3,2,1,0:T(4,128)(2,1)S(1)}, u32[]{:S(2)}, u32[]{:S(2)}) %all-to-all-start.2) | async-done | bytes 1048608 | tf_op jit(solution)/shard_map/all_to_all | solution.py:99
  110.0 4.2 %all-to-all-start.3 = ((bf16[8,128,4,128]{3,2,1,0:T(4,128)(2,1)}), bf16[8,128,4,128]{3,2,1,0:T(4,128)(2,1)}, u32[]{:S(2)}, u32[]{:S(2)}) async-start(bf16[8,128,4,128]{3,2,1,0:T(4,128)(2,1)} %bitcast.34), calls=%async_computation.3 | async-start | bytes 2097152 | tf_op jit(solution)/shard_map/all_to_all | solution.py:99
  114.2 1.9 collective-permute-start.1
  117.8 2.3 collective-permute-start
  121.2 21.1 %collective-permute-done.1 = bf16[32,128,128]{2,1,0:T(8,128)(2,1)S(1)} collective-permute-done((bf16[32,128,128]{2,1,0:T(8,128)(2,1)}, bf16[32,128,128]{2,1,0:T(8,128)(2,1)S(1)}, u32[]{:S(2)}, u32[]{:S(2)}) %collective-permute-start.1) | collective-permute-done | bytes 1048608 | tf_op jit(solution)/shard_map/ppermute | solution.py:114
  142.4 2.8 pad_maximum_fusion.1.vals
  145.1 19.0 %collective-permute-done = bf16[32,128,128]{2,1,0:T(8,128)(2,1)} collective-permute-done((bf16[32,128,128]{2,1,0:T(8,128)(2,1)}, bf16[32,128,128]{2,1,0:T(8,128)(2,1)}, u32[]{:S(2)}, u32[]{:S(2)}) %collective-permute-start) | collective-permute-done | bytes 1048608 | tf_op jit(solution)/shard_map/ppermute | solution.py:114
  165.5 14.3 %grads.1 = (bf16[8,512,128]{2,1,0:T(8,128)(2,1)S(1)}, f32[64,128,128]{2,1,0:T(8,128)}, f32[64,128,128]{2,1,0:T(8,128)}) custom-call(s32[8,5]{1,0:T(8,128)S(1)} %fusion.3.idx, f32[8,5]{1,0:T(8,128)S(1)} %compare_select_fusion.bias, f32[8,1,512]{2,1,0:T(1,128)S(1)} %copy.34.lse, f32[8,1,512]{2,1,0:T(1,128)S(1)} %copy.35.delta, ...), custom_call_target="tpu_custom_call" | custom-call | flops 3355443200 | bytes 12582912 | tf_op jit(solution)/shard_map/grads/pallas_call | solution.py:68
  180.8 6.8 %all-to-all-start.6 = ((bf16[8,128,4,128]{3,2,1,0:T(4,128)(2,1)}), bf16[8,128,4,128]{3,2,1,0:T(4,128)(2,1)S(1)}, u32[]{:S(2)}, u32[]{:S(2)}) async-start(bf16[8,128,4,128]{3,2,1,0:T(4,128)(2,1)} %bitcast.39), calls=%async_computation.6 | async-start | bytes 2097152 | tf_op jit(solution)/shard_map/all_to_all | solution.py:99
  189.3 2.8 collective-permute-start.3
  192.1 25.0 %collective-permute-done.3 = bf16[32,128,128]{2,1,0:T(8,128)(2,1)S(1)} collective-permute-done((bf16[32,128,128]{2,1,0:T(8,128)(2,1)S(1)}, bf16[32,128,128]{2,1,0:T(8,128)(2,1)S(1)}, u32[]{:S(2)}, u32[]{:S(2)}) %collective-permute-start.3) | collective-permute-done | bytes 1048608 | tf_op jit(solution)/shard_map/ppermute | solution.py:145
  217.1 2.9 add_convert_fusion
  220.0 3.5 %all-to-all-start.9 = ((bf16[32,128,128]{2,1,0:T(8,128)(2,1)}), bf16[32,128,128]{2,1,0:T(8,128)(2,1)S(1)}, u32[]{:S(2)}, u32[]{:S(2)}) async-start(bf16[32,128,128]{2,1,0:T(8,128)(2,1)} %add_convert_fusion), calls=%async_computation.9 | async-start | bytes 2097152 | tf_op jit(solution)/shard_map/all_to_all | solution.py:99
  225.3 1.9 collective-permute-start.2
  227.2 43.4 %collective-permute-done.2 = bf16[32,128,128]{2,1,0:T(8,128)(2,1)S(1)} collective-permute-done((bf16[32,128,128]{2,1,0:T(8,128)(2,1)S(1)}, bf16[32,128,128]{2,1,0:T(8,128)(2,1)S(1)}, u32[]{:S(2)}, u32[]{:S(2)}) %collective-permute-start.2) | collective-permute-done | bytes 1048608 | tf_op jit(solution)/shard_map/ppermute | solution.py:145
  270.6 2.9 add_convert_fusion.1
  273.5 6.8 %all-to-all-start.7 = ((bf16[32,128,128]{2,1,0:T(8,128)(2,1)}), bf16[32,128,128]{2,1,0:T(8,128)(2,1)S(1)}, u32[]{:S(2)}, u32[]{:S(2)}) async-start(bf16[32,128,128]{2,1,0:T(8,128)(2,1)} %add_convert_fusion.1), calls=%async_computation.7 | async-start | bytes 2097152 | tf_op jit(solution)/shard_map/all_to_all | solution.py:99
  281.3 25.9 %all-to-all-done.7 = bf16[32,128,128]{2,1,0:T(8,128)(2,1)S(1)} async-done(((bf16[32,128,128]{2,1,0:T(8,128)(2,1)}), bf16[32,128,128]{2,1,0:T(8,128)(2,1)S(1)}, u32[]{:S(2)}, u32[]{:S(2)}) %all-to-all-start.7) | async-done | bytes 1048608 | tf_op jit(solution)/shard_map/all_to_all | solution.py:99
  307.1 6.9 %all-to-all-start.10 = ((bf16[8,128,128]{2,1,0:T(8,128)(2,1)}), bf16[8,128,128]{2,1,0:T(8,128)(2,1)S(1)}, u32[]{:S(2)}, u32[]{:S(2)}) async-start(bf16[8,128,128]{2,1,0:T(8,128)(2,1)} %reduce_sum.25), calls=%async_computation.10 | async-start | bytes 524288 | tf_op jit(solution)/shard_map/all_to_all | solution.py:99
  315.0 9.6 %all-to-all-done.10 = bf16[8,128,128]{2,1,0:T(8,128)(2,1)S(1)} async-done(((bf16[8,128,128]{2,1,0:T(8,128)(2,1)}), bf16[8,128,128]{2,1,0:T(8,128)(2,1)S(1)}, u32[]{:S(2)}, u32[]{:S(2)}) %all-to-all-start.10) | async-done | bytes 262176 | tf_op jit(solution)/shard_map/all_to_all | solution.py:99
  324.5 3.4 all-to-all-start.8
  330.2 8.2 %all-to-all-done.8 = bf16[8,128,128]{2,1,0:T(8,128)(2,1)S(1)} async-done(((bf16[8,128,128]{2,1,0:T(8,128)(2,1)}), bf16[8,128,128]{2,1,0:T(8,128)(2,1)S(1)}, u32[]{:S(2)}, u32[]{:S(2)}) %all-to-all-start.8) | async-done | bytes 262176 | tf_op jit(solution)/shard_map/all_to_all | solution.py:99
  (48 shorter events, 21.4 us)
Async XLA Ops:
  7.2 113.0 %copy-start = (s32[512,5]{0,1:T(8,128)S(1)}, s32[512,5]{0,1:T(8,128)}, u32[]{:S(2)}) copy-start(s32[512,5]{0,1:T(8,128)} %param.13) | copy-start | bytes 30724
  7.2 57.7 %copy-start.2 = (bf16[128,32,128]{2,1,0:T(8,128)(2,1)S(1)}, bf16[128,32,128]{2,1,0:T(8,128)(2,1)}, u32[]{:S(2)}) copy-start(bf16[128,32,128]{2,1,0:T(8,128)(2,1)} %param.7) | copy-start | bytes 3145732
  9.0 19.0 %all-to-all-start.5 = ((bf16[8,128,128]{2,1,0:T(8,128)(2,1)}), bf16[8,128,128]{2,1,0:T(8,128)(2,1)S(1)}, u32[]{:S(2)}, u32[]{:S(2)}) async-start(bf16[8,128,128]{2,1,0:T(8,128)(2,1)} %bitcast.36), calls=%async_computation.5 | async-start | bytes 524288 | tf_op jit(solution)/shard_map/all_to_all | solution.py:99
  16.1 98.2 %all-gather.5.cloned.1.call-start = ((), (), s32[]{:S(2)}) async-start(), calls=%async_computation.12 | async-start | bytes 1310720 | tf_op jit(solution)/shard_map/all_gather | solution.py:111
  27.9 0.7 copy-start.4
  30.0 18.0 %all-to-all-start = ((f32[4,8,128]{2,1,0:T(8,128)}), f32[4,8,128]{2,1,0:T(8,128)S(1)}, u32[]{:S(2)}, u32[]{:S(2)}) async-start(f32[4,8,128]{2,1,0:T(8,128)} %copy.26), calls=%async_computation | async-start | bytes 32768 | tf_op jit(solution)/shard_map/all_to_all | solution.py:99
  48.1 13.3 %all-to-all-start.1 = ((f32[4,8,128]{2,1,0:T(8,128)}), f32[4,8,128]{2,1,0:T(8,128)S(1)}, u32[]{:S(2)}, u32[]{:S(2)}) async-start(f32[4,8,128]{2,1,0:T(8,128)} %copy.28), calls=%async_computation.1 | async-start | bytes 32768 | tf_op jit(solution)/shard_map/all_to_all | solution.py:99
  61.4 15.8 %all-to-all-start.4 = ((bf16[8,128,128]{2,1,0:T(8,128)(2,1)}), bf16[8,128,128]{2,1,0:T(8,128)(2,1)S(1)}, u32[]{:S(2)}, u32[]{:S(2)}) async-start(bf16[8,128,128]{2,1,0:T(8,128)(2,1)} %bitcast.37), calls=%async_computation.4 | async-start | bytes 524288 | tf_op jit(solution)/shard_map/all_to_all | solution.py:99
  64.9 16.7 %copy-start.3 = (bf16[128,32,128]{2,1,0:T(8,128)(2,1)S(1)}, bf16[128,32,128]{2,1,0:T(8,128)(2,1)}, u32[]{:S(2)}) copy-start(bf16[128,32,128]{2,1,0:T(8,128)(2,1)} %param.10) | copy-start | bytes 3145732
  77.2 3.6 %copy-start.5 = (bf16[8,128,128]{2,1,0:T(8,128)(2,1)}, bf16[8,128,128]{2,1,0:T(8,128)(2,1)S(1)}, u32[]{:S(2)}) copy-start(bf16[8,128,128]{2,1,0:T(8,128)(2,1)S(1)} %all-to-all-done.4) | copy-start | bytes 786436
  77.2 32.7 %all-to-all-start.2 = ((bf16[8,128,4,128]{3,2,1,0:T(4,128)(2,1)}), bf16[8,128,4,128]{3,2,1,0:T(4,128)(2,1)S(1)}, u32[]{:S(2)}, u32[]{:S(2)}) async-start(bf16[8,128,4,128]{3,2,1,0:T(4,128)(2,1)} %bitcast.35), calls=%async_computation.2 | async-start | bytes 2097152 | tf_op jit(solution)/shard_map/all_to_all | solution.py:99
  80.8 37.0 %all-gather.3.cloned.1.call-start = ((), (), s32[]{:S(2)}) async-start(), calls=%async_computation.11 | async-start | bytes 1310720 | tf_op jit(solution)/shard_map/all_gather | solution.py:111
  110.0 55.6 %all-to-all-start.3 = ((bf16[8,128,4,128]{3,2,1,0:T(4,128)(2,1)}), bf16[8,128,4,128]{3,2,1,0:T(4,128)(2,1)}, u32[]{:S(2)}, u32[]{:S(2)}) async-start(bf16[8,128,4,128]{3,2,1,0:T(4,128)(2,1)} %bitcast.34), calls=%async_computation.3 | async-start | bytes 2097152 | tf_op jit(solution)/shard_map/all_to_all | solution.py:99
  114.2 28.1 %collective-permute-start.1 = (bf16[32,128,128]{2,1,0:T(8,128)(2,1)}, bf16[32,128,128]{2,1,0:T(8,128)(2,1)S(1)}, u32[]{:S(2)}, u32[]{:S(2)}) collective-permute-start(bf16[32,128,128]{2,1,0:T(8,128)(2,1)} %all-gather.5.cloned.1.call-done), channel_id=1, source_target_pairs={{0,1},{1,2},{2,3},{3,4},{4,5},{5,6},{6,7},{7,8},{8,9},{9,10},{10,1... | collective-permute-start | bytes 3145736 | tf_op jit(solution)/shard_map/ppermute | solution.py:114
  117.8 46.3 %collective-permute-start = (bf16[32,128,128]{2,1,0:T(8,128)(2,1)}, bf16[32,128,128]{2,1,0:T(8,128)(2,1)}, u32[]{:S(2)}, u32[]{:S(2)}) collective-permute-start(bf16[32,128,128]{2,1,0:T(8,128)(2,1)} %all-gather.3.cloned.1.call-done), channel_id=1, source_target_pairs={{0,1},{1,2},{2,3},{3,4},{4,5},{5,6},{6,7},{7,8},{8,9},{9,10},{10,1... | collective-permute-start | bytes 3145736 | tf_op jit(solution)/shard_map/ppermute | solution.py:114
  121.2 42.9 %copy-start.6 = (bf16[32,128,128]{2,1,0:T(8,128)(2,1)S(1)}, bf16[32,128,128]{2,1,0:T(8,128)(2,1)}, u32[]{:S(2)}) copy-start(bf16[32,128,128]{2,1,0:T(8,128)(2,1)} %all-gather.3.cloned.1.call-done) | copy-start | bytes 3145732
  179.8 1.0 copy-start.1
  180.8 39.3 %all-to-all-start.6 = ((bf16[8,128,4,128]{3,2,1,0:T(4,128)(2,1)}), bf16[8,128,4,128]{3,2,1,0:T(4,128)(2,1)S(1)}, u32[]{:S(2)}, u32[]{:S(2)}) async-start(bf16[8,128,4,128]{3,2,1,0:T(4,128)(2,1)} %bitcast.39), calls=%async_computation.6 | async-start | bytes 2097152 | tf_op jit(solution)/shard_map/all_to_all | solution.py:99
  189.3 27.8 %collective-permute-start.3 = (bf16[32,128,128]{2,1,0:T(8,128)(2,1)S(1)}, bf16[32,128,128]{2,1,0:T(8,128)(2,1)S(1)}, u32[]{:S(2)}, u32[]{:S(2)}) collective-permute-start(bf16[32,128,128]{2,1,0:T(8,128)(2,1)S(1)} %slice.29), channel_id=1, source_target_pairs={{1,0},{2,1},{3,2},{4,3},{5,4},{6,5},{7,6},{8,7},{9,8},{10,9},{11,1... | collective-permute-start | bytes 3145736 | tf_op jit(solution)/shard_map/ppermute | solution.py:145
  220.0 53.5 %all-to-all-start.9 = ((bf16[32,128,128]{2,1,0:T(8,128)(2,1)}), bf16[32,128,128]{2,1,0:T(8,128)(2,1)S(1)}, u32[]{:S(2)}, u32[]{:S(2)}) async-start(bf16[32,128,128]{2,1,0:T(8,128)(2,1)} %add_convert_fusion), calls=%async_computation.9 | async-start | bytes 2097152 | tf_op jit(solution)/shard_map/all_to_all | solution.py:99
  225.3 45.3 %collective-permute-start.2 = (bf16[32,128,128]{2,1,0:T(8,128)(2,1)S(1)}, bf16[32,128,128]{2,1,0:T(8,128)(2,1)S(1)}, u32[]{:S(2)}, u32[]{:S(2)}) collective-permute-start(bf16[32,128,128]{2,1,0:T(8,128)(2,1)S(1)} %slice.30), channel_id=1, source_target_pairs={{1,0},{2,1},{3,2},{4,3},{5,4},{6,5},{7,6},{8,7},{9,8},{10,9},{11,1... | collective-permute-start | bytes 3145736 | tf_op jit(solution)/shard_map/ppermute | solution.py:145
  273.5 33.6 %all-to-all-start.7 = ((bf16[32,128,128]{2,1,0:T(8,128)(2,1)}), bf16[32,128,128]{2,1,0:T(8,128)(2,1)S(1)}, u32[]{:S(2)}, u32[]{:S(2)}) async-start(bf16[32,128,128]{2,1,0:T(8,128)(2,1)} %add_convert_fusion.1), calls=%async_computation.7 | async-start | bytes 2097152 | tf_op jit(solution)/shard_map/all_to_all | solution.py:99
  307.1 17.4 %all-to-all-start.10 = ((bf16[8,128,128]{2,1,0:T(8,128)(2,1)}), bf16[8,128,128]{2,1,0:T(8,128)(2,1)S(1)}, u32[]{:S(2)}, u32[]{:S(2)}) async-start(bf16[8,128,128]{2,1,0:T(8,128)(2,1)} %reduce_sum.25), calls=%async_computation.10 | async-start | bytes 524288 | tf_op jit(solution)/shard_map/all_to_all | solution.py:99
  324.5 13.8 %all-to-all-start.8 = ((bf16[8,128,128]{2,1,0:T(8,128)(2,1)}), bf16[8,128,128]{2,1,0:T(8,128)(2,1)S(1)}, u32[]{:S(2)}, u32[]{:S(2)}) async-start(bf16[8,128,128]{2,1,0:T(8,128)(2,1)} %reduce_sum.24), calls=%async_computation.8 | async-start | bytes 524288 | tf_op jit(solution)/shard_map/all_to_all | solution.py:99
Sparse Core Ops, SparseCore 0:
  28.8 34.4 all-gather.4
  84.3 33.4 all-gather.2

commit v2 on v1

v2 whole, which is shorter than its diff:
```python
import functools
import math

import jax
import jax.numpy as jnp
from jax import lax
from jax.experimental import pallas as pl
from jax.experimental.pallas import tpu as pltpu
from jax.sharding import PartitionSpec as P

BLOCK = 128
OFF = -1e30
MESH = pl.DeviceIdType.MESH
NEAR_FIRST = (0, 1, 7, 2, 6, 3, 5, 4)


class Place:
    def __init__(self, uly, blks, rows):
        self.fold = uly // rows
        self.rows = rows
        self.u, self.slab = lax.axis_index("uly"), lax.axis_index("blk")
        self.y, self.r = self.u // self.fold, self.u % self.fold
        self.z, self.c = self.r // 2, self.r % 2
        self.first, self.last = self.slab == 0, self.slab == blks - 1
        self.core = self.at(self.z * 2 + 1 - self.c)
        self.other = self.at((1 - self.z) * 2 + self.c)
        self.cross = self.at((1 - self.z) * 2 + 1 - self.c)
        self.after, self.before = {"blk": self.slab + 1}, {"blk": self.slab - 1}

    def at(self, r):
        return {"uly": self.y * self.fold + r}

    def row(self, y):
        return {"uly": y * self.fold + self.r}

    def y_at(self, distance):
        return (self.y + distance) % self.rows

    def meet(self):
        barrier = pltpu.get_barrier_semaphore()

        def greet(device):
            pl.semaphore_signal(barrier, inc=1, device_id=device, device_id_type=MESH)

        for d in range(1, self.rows):
            greet(self.row(self.y_at(d)))
        for device in (self.core, self.other, self.cross):
            greet(device)
        pl.when(jnp.logical_not(self.last))(lambda: greet(self.after))
        pl.when(jnp.logical_not(self.first))(lambda: greet(self.before))
        ends = self.first.astype(jnp.int32) + self.last.astype(jnp.int32)
        pl.semaphore_wait(barrier, self.rows + 4 - ends)


def remote(src, dst, sems, i, device):
    return pltpu.make_async_remote_copy(
        src_ref=src,
        dst_ref=dst,
        send_sem=sems[0].at[i],
        recv_sem=sems[1].at[i],
        device_id=device,
        device_id_type=MESH,
    )


def pair(n):
    return [pltpu.SemaphoreType.DMA((n,)), pltpu.SemaphoreType.DMA((n,))]


def inbound_kernel(uly, blks, q, do, kv, lse, delta, q_all, do_all, kv_all, lse_all, delta_all, *sems):
    rows = kv.shape[0]
    q_s, do_s, kv_s, z_s, x_s, c_s, l_s, e_s = [sems[2 * i : 2 * i + 2] for i in range(8)]
    own = sems[16]
    me = Place(uly, blks, rows)
    y, r, z, c = me.y, me.r, me.z, me.c
    has_after, has_before = jnp.logical_not(me.last), jnp.logical_not(me.first)
    me.meet()

    locals_ = [
        pltpu.make_async_copy(kv.at[y], kv_all.at[c, 1, z, y], own.at[0]),
        pltpu.make_async_copy(q.at[:, y], q_all.at[y], own.at[1]),
        pltpu.make_async_copy(do.at[:, y], do_all.at[y], own.at[2]),
        pltpu.make_async_copy(lse.at[r], lse_all.at[r], own.at[3]),
        pltpu.make_async_copy(delta.at[r], delta_all.at[r], own.at[4]),
    ]
    sends = []
    for d in range(1, rows):
        t = me.y_at(d)
        sends.append(remote(kv.at[t], kv_all.at[c, 1, z, y], kv_s, d, me.row(t)))
    for d in range(1, rows):
        t = me.y_at(d)
        sends.append(remote(q.at[:, t], q_all.at[y], q_s, d, me.row(t)))
        sends.append(remote(do.at[:, t], do_all.at[y], do_s, d, me.row(t)))
    for i in range(1, me.fold):
        t = (r + i) % me.fold
        sends.append(remote(lse.at[t], lse_all.at[r], l_s, i, me.at(t)))
        sends.append(remote(delta.at[t], delta_all.at[r], e_s, i, me.at(t)))
    for copy in locals_ + sends:
        copy.start()

    def from_row(d):
        place = kv_all.at[c, 1, z, me.y_at(rows - d)]
        return remote(place, place, kv_s, d, me.core)

    def to_other(d):
        place = kv_all.at[c, 1, z, me.y_at(rows - d)]
        return remote(place, place, z_s, d, me.other)

    def from_other(d):
        place = kv_all.at[c, 1, 1 - z, me.y_at(rows - d)]
        return remote(place, place, z_s, d, me.other)

    def to_after(d, zz, i):
        t = me.y_at(rows - d)
        return remote(kv_all.at[c, 1, zz, t], kv_all.at[c, 0, zz, t], x_s, i, me.after)

    def from_before(d, zz, i):
        place = kv_all.at[c, 0, zz, me.y_at(rows - d)]
        return remote(place, place, x_s, i, me.before)

    def to_core(d, part, zz, i):
        place = kv_all.at[c, part, zz, me.y_at(rows - d)]
        return remote(place, place, c_s, i, me.core)

    def from_core(d, part, zz, i):
        place = kv_all.at[1 - c, part, zz, me.y_at(rows - d)]
        return remote(place, place, c_s, i, me.core)

    for d in NEAR_FIRST:
        if d == 0:
            locals_[0].wait()
        else:
            from_row(d).wait_recv()
        to_other(d).start()
        pl.when(has_after)(lambda: to_after(d, z, d).start())
        to_core(d, 1, z, d).start()
    for d in NEAR_FIRST:
        from_other(d).wait_recv()
        pl.when(has_after)(lambda: to_after(d, 1 - z, rows + d).start())
        to_core(d, 1, 1 - z, rows + d).start()

        @pl.when(has_before)
        def _():
            from_before(d, z, d).wait_recv()
            to_core(d, 0, z, 2 * rows + d).start()

    @pl.when(has_before)
    def _():
        for d in NEAR_FIRST:
            from_before(d, 1 - z, rows + d).wait_recv()
            to_core(d, 0, 1 - z, 3 * rows + d).start()

    for copy in sends:
        copy.wait_send()
    for d in range(1, rows):
        q_piece, do_piece = q_all.at[me.y_at(rows - d)], do_all.at[me.y_at(rows - d)]
        remote(q_piece, q_piece, q_s, d, me.core).wait_recv()
        remote(do_piece, do_piece, do_s, d, me.core).wait_recv()
    for i in range(1, me.fold):
        t = (r + me.fold - i) % me.fold
        remote(lse_all.at[t], lse_all.at[t], l_s, i, me.core).wait_recv()
        remote(delta_all.at[t], delta_all.at[t], e_s, i, me.core).wait_recv()
    for copy in locals_[1:]:
        copy.wait()
    for d in range(rows):
        to_other(d).wait_send()
        for zz, base in ((z, 0), (1 - z, rows)):
            pl.when(has_after)(lambda: to_after(d, zz, base + d).wait_send())
            to_core(d, 1, zz, base + d).wait_send()
            from_core(d, 1, zz, base + d).wait_recv()

            @pl.when(has_before)
            def _():
                to_core(d, 0, zz, 2 * rows + base + d).wait_send()
                from_core(d, 0, zz, 2 * rows + base + d).wait_recv()


def inbound(uly, blks, q, do, kv, lse, delta):
    tokens, rows, group, hd = q.shape
    any_ = pl.BlockSpec(memory_space=pltpu.HBM)
    parts = jax.ShapeDtypeStruct((rows, tokens, group, hd), q.dtype)
    every = jax.ShapeDtypeStruct((2, 2, 2) + kv.shape, kv.dtype)
    scalars = jax.ShapeDtypeStruct(lse.shape, lse.dtype)
    return pl.pallas_call(
        functools.partial(inbound_kernel, uly, blks),
        out_shape=(parts, parts, every, scalars, scalars),
        in_specs=[any_] * 5,
        out_specs=(any_,) * 5,
        scratch_shapes=pair(rows) * 4
        + pair(2 * rows)
        + pair(4 * rows)
        + pair(4) * 2
        + [pltpu.SemaphoreType.DMA((5,))],
        compiler_params=pltpu.CompilerParams(collective_id=0, has_side_effects=True),
        name="inbound",
    )(q, do, kv, lse, delta)


def outbound_kernel(uly, blks, dq, mine, theirs, grad_q, home, from_c, to_x, from_x, to_z, from_z, total, to_y, *sems):
    rows = dq.shape[0]
    q_s, c_s, x_s, z_s, y_s = [sems[2 * i : 2 * i + 2] for i in range(5)]
    own = sems[10]
    me = Place(uly, blks, rows)
    y, z = me.y, me.z
    has_after, has_before = jnp.logical_not(me.last), jnp.logical_not(me.first)
    me.meet()

    def core(part, zz, order, d):
        t = me.y_at(d)
        i = (part * 2 + order) * rows + d
        return remote(theirs.at[part, zz, t], from_c.at[part, zz, t], c_s, i, me.core)

    def before(zz, order, d):
        t = me.y_at(d)
        return remote(to_x.at[zz, t], from_x.at[zz, t], x_s, order * rows + d, me.before)

    def other(d):
        t = me.y_at(d)
        return remote(to_z.at[t], from_z.at[t], z_s, d, me.other)

    ways = ((1 - z, 0), (z, 1))
    for part in (0, 1):
        for zz, order in ways:
            for d in range(rows):
                core(part, zz, order, d).start()
    keep = pltpu.make_async_copy(dq.at[y], grad_q.at[:, y], own.at[0])
    keep.start()
    sends = []
    for d in range(1, rows):
        t = me.y_at(d)
        sends.append(remote(dq.at[t], grad_q.at[:, y], q_s, d, me.row(t)))
        sends[-1].start()

    for zz, order in ways:

        @pl.loop(0, rows)
        def _(d):
            t = me.y_at(d)
            core(0, zz, order, d).wait_recv()

            @pl.when(has_before)
            def _():
                to_x[zz, t] = (mine[0, zz, t] + from_c[0, zz, t]).astype(jnp.bfloat16)
                before(zz, order, d).start()

    def summed(zz, order, d, store):
        t = me.y_at(d)
        core(1, zz, order, d).wait_recv()

        @pl.when(has_after)
        def _():
            before(zz, order, d).wait_recv()
            store(t, mine[1, zz, t] + from_c[1, zz, t] + from_x[zz, t])

        @pl.when(me.last)
        def _():
            store(t, mine[1, zz, t] + from_c[1, zz, t])

    @pl.loop(0, rows)
    def _(d):
        def store(t, x):
            to_z[t] = x.astype(jnp.bfloat16)

        summed(1 - z, 0, d, store)
        other(d).start()

    def back(d):
        t = me.y_at(d)
        return remote(to_y.at[t], home.at[y], y_s, d, me.row(t))

    @pl.loop(0, rows)
    def _(d):
        def store(t, x):
            total[...] = x

        summed(z, 1, d, store)
        other(d).wait_recv()
        t = me.y_at(d)
        to_y[t] = (total[...] + from_z[t]).astype(jnp.bfloat16)
        pl.when(d > 0)(lambda: back(d).start())

    last = pltpu.make_async_copy(to_y.at[y], home.at[y], own.at[1])
    last.start()
    for d in range(rows):
        for part in (0, 1):
            for zz, order in ways:
                core(part, zz, order, d).wait_send()
        for zz, order in ways:
            pl.when(has_before)(lambda: before(zz, order, d).wait_send())
        other(d).wait_send()
    for d in range(1, rows):
        t = me.y_at(rows - d)
        sends[d - 1].wait_send()
        remote(dq.at[t], grad_q.at[:, t], q_s, d, me.core).wait_recv()
        back(d).wait_send()
        remote(to_y.at[t], home.at[t], y_s, d, me.core).wait_recv()
    keep.wait()
    last.wait()


def outbound(uly, blks, dq, mine, theirs):
    rows, tokens, group, hd = dq.shape
    hbm, vmem = pl.BlockSpec(memory_space=pltpu.HBM), pl.BlockSpec(memory_space=pltpu.VMEM)
    piece = mine.shape[3:]
    low = jnp.bfloat16
    return pl.pallas_call(
        functools.partial(outbound_kernel, uly, blks),
        out_shape=(
            jax.ShapeDtypeStruct((tokens, rows, group, hd), low),
            jax.ShapeDtypeStruct((rows,) + piece, low),
        ),
        in_specs=[hbm, vmem, hbm],
        out_specs=(hbm, hbm),
        scratch_shapes=[
            pltpu.VMEM(mine.shape, low),
            pltpu.VMEM(mine.shape[1:], low),
            pltpu.VMEM(mine.shape[1:], low),
            pltpu.VMEM((rows,) + piece, low),
            pltpu.VMEM((rows,) + piece, low),
            pltpu.VMEM(piece, jnp.float32),
            pltpu.VMEM((rows,) + piece, low),
        ]
        + pair(rows)
        + pair(4 * rows)
        + pair(2 * rows)
        + pair(rows) * 2
        + [pltpu.SemaphoreType.DMA((2,))],
        compiler_params=pltpu.CompilerParams(
            collective_id=1, has_side_effects=True, vmem_limit_bytes=32 << 20
        ),
        name="outbound",
    )(dq, mine, theirs)


def grads_kernel(scale, idx, bias, half, lse, delta, q, do, kv, dq, mine, theirs, acc):
    step = pl.program_id(0)
    select = idx.shape[1]
    rows = q.shape[1]
    heads = rows // BLOCK

    @pl.when(step == 0)
    def _():
        acc[...] = jnp.zeros_like(acc)

    places = [idx[step, j] for j in range(select)]
    kcat = jnp.concatenate([kv[c, 0] for c in places], 0)
    vcat = jnp.concatenate([kv[c, 1] for c in places], 0)
    qb, dob = q[0], do[0]
    nt = (((1,), (1,)), ((), ()))
    nn = (((1,), (0,)), ((), ()))
    s = lax.dot_general(kcat, qb, nt, preferred_element_type=jnp.float32)
    dp = lax.dot_general(vcat, dob, nt, preferred_element_type=jnp.float32)
    lse_row, delta_row = lse[0], delta[0]
    probs, dscores = [], []
    for j in range(select):
        part = slice(j * BLOCK, (j + 1) * BLOCK)
        p = jnp.exp(s[part] * scale - (lse_row - bias[step, j]))
        if j == 0:
            key_at = lax.broadcasted_iota(jnp.int32, (BLOCK, rows), 0)
            query_at = lax.broadcasted_iota(jnp.int32, (BLOCK, rows), 1) // heads
            p = jnp.where(key_at <= query_at, p, 0.0)
        ds = p * (dp[part] - delta_row)
        probs.append(p.astype(jnp.bfloat16))
        dscores.append(ds.astype(jnp.bfloat16))
    pcat = jnp.concatenate(probs, 0)
    dscat = jnp.concatenate(dscores, 0)
    dv_part = lax.dot_general(pcat, dob, nn, preferred_element_type=jnp.float32)
    dk_part = lax.dot_general(dscat, qb, nn, preferred_element_type=jnp.float32)
    dqt = lax.dot_general(kcat.T, dscat, nn, preferred_element_type=jnp.float32)
    dq[0] = (dqt * scale).T.astype(jnp.bfloat16)
    for j, c in enumerate(places):
        part = slice(j * BLOCK, (j + 1) * BLOCK)
        acc[c, 0] += dk_part[part] * scale
        acc[c, 1] += dv_part[part]

    @pl.when(step == pl.num_programs(0) - 1)
    def _():
        count = mine.shape[0]
        mine[...] = acc[pl.ds(half[0] * count, count)]
        theirs[...] = acc[pl.ds((1 - half[0]) * count, count)].astype(jnp.bfloat16)


def local_grads(idx, bias, half, lse, delta, q, do, kv):
    steps, rows, hd = q.shape
    places = kv.shape[0]
    select = idx.shape[1]
    row = pl.BlockSpec((1, 1, rows), lambda i, *_: (i, 0, 0))
    tile = pl.BlockSpec((1, rows, hd), lambda i, *_: (i, 0, 0))

    def whole(n):
        return pl.BlockSpec(
            (n, 2, BLOCK, hd), lambda i, *_: (0, 0, 0, 0), pipeline_mode=pl.Buffered(1)
        )

    part = (places // 2, 2, BLOCK, hd)
    return pl.pallas_call(
        functools.partial(grads_kernel, 1.0 / math.sqrt(hd)),
        out_shape=(
            jax.ShapeDtypeStruct(q.shape, jnp.bfloat16),
            jax.ShapeDtypeStruct(part, jnp.float32),
            jax.ShapeDtypeStruct(part, jnp.bfloat16),
        ),
        grid_spec=pltpu.PrefetchScalarGridSpec(
            num_scalar_prefetch=3,
            grid=(steps,),
            in_specs=[row, row, tile, tile, whole(places)],
            out_specs=(tile, whole(places // 2), whole(places // 2)),
            scratch_shapes=[pltpu.VMEM((places, 2, BLOCK, hd), jnp.float32)],
        ),
        compiler_params=pltpu.CompilerParams(vmem_limit_bytes=48 << 20),
        name="grads",
    )(idx, bias, half, lse, delta, q, do, kv)


def shards(queries, keys, values, grad_out, lse, delta, block_keys):
    uly, blks = lax.axis_size("uly"), lax.axis_size("blk")
    tokens, heads, hd = queries.shape
    kvh = keys.shape[1]
    group = heads // kvh
    fold = uly // kvh
    u, slab = lax.axis_index("uly"), lax.axis_index("blk")
    slab_len = uly * tokens

    def mine_of(x):
        x = lax.dynamic_slice_in_dim(x, slab * slab_len, slab_len, 1)
        return x.reshape(kvh, fold, tokens).transpose(1, 0, 2)

    kv = jnp.stack([keys, values], 0).transpose(2, 0, 1, 3)
    q, do, kv, lse_rows, delta_rows = inbound(
        uly,
        blks,
        queries.reshape(tokens, kvh, group, hd),
        grad_out.reshape(tokens, kvh, group, hd),
        kv,
        mine_of(lse),
        mine_of(delta),
    )

    def rows_of(x):
        return x.transpose(1, 2, 0).reshape(kvh, 1, tokens * group)

    own_blocks = lax.dynamic_slice_in_dim(block_keys, slab * uly, uly, 0)
    own_blocks = lax.dynamic_index_in_dim(
        own_blocks.reshape(kvh, fold, -1), u % fold, 1, keepdims=False
    )
    own_at = jnp.where(own_blocks >= 0, own_blocks, own_blocks[:, :1])
    rel = own_at - (slab - 1) * uly
    part, home = rel // uly, rel % uly
    y, z, c = home // fold, home % fold // 2, home % 2
    idx = ((c * 2 + part) * 2 + z) * kvh + y
    bias = jnp.where(own_blocks >= 0, 0.0, OFF).astype(jnp.float32)

    dq, mine, theirs = local_grads(
        idx,
        bias,
        (u % 2).reshape(1).astype(jnp.int32),
        rows_of(lse_rows),
        rows_of(delta_rows),
        q.reshape(kvh, tokens * group, hd),
        do.reshape(kvh, tokens * group, hd),
        kv.reshape(uly * 2, 2, tokens, hd),
    )
    part = (2, 2, kvh, 2, tokens, hd)
    grad_q, home = outbound(
        uly,
        blks,
        dq.reshape(kvh, tokens, group, hd),
        mine.reshape(part),
        theirs.reshape(part),
    )
    home = home.transpose(1, 2, 0, 3)
    return grad_q.reshape(tokens, heads, hd), home[0], home[1]


def solution(mesh):
    data = P(("blk", "uly"), None, None)
    return jax.shard_map(
        shards,
        mesh=mesh,
        in_specs=(data, data, data, data, P("uly", None), P("uly", None), P()),
        out_specs=(data, data, data),
        check_vma=False,
    )
```

time: 349 us -> 165 us (0.47)
  the two profiles are of different devices: /device:TPU:6 before, /device:TPU:193 now
where the time goes in v2:
time: 165 us
  Pallas kernels  149 us (90%)
  local copies, waits for them, and re-layouts  13.6 us (8%)
    pallas_call x1, Pallas kernels, inbound(): pl.pallas_call(functools.partial(inbound_kernel, uly, blks), out_shape=(p...  67.8 us
    pallas_call x1, Pallas kernels, outbound(): pl.pallas_call(functools.partial(outbound_kernel, uly, blks), out_shape=(...  67.5 us
    pallas_call x1, Pallas kernels, local_grads(): pl.pallas_call(functools.partial(grads_kernel, 1.0 / math.sqrt(hd)), out_...  14.1 us
    unnamed x11, local copies, waits for them, and re-layouts  8.06 us

profile of v2, /device:TPU:193, one launch (start us, length us, event | category | flops | bytes accessed | tf_op | source)
XLA Modules:
  0.0 164.7 jit_solution(15136328395169871637)
XLA Ops:
  0.6 0.0 copy-start
  0.7 0.7 copy-done
  1.4 0.1 constant_dynamic-slice_fusion.3
  1.4 0.1 reshape.51
  1.5 0.1 constant_dynamic-slice_fusion.2
  1.6 0.1 copy.16
  1.7 0.1 slice_reduce_fusion
  1.8 0.1 fusion.6.idx
  2.0 0.7 constant_dynamic-slice_fusion
  2.7 0.6 copy.31
  3.3 0.6 copy.32
  3.9 1.1 copy_bitcast_fusion
  5.0 0.8 maximum_bitcast_fusion.kv
  5.9 67.8 %inbound.1 = (bf16[8,128,4,128]{3,2,1,0:T(4,128)(2,1)}, bf16[8,128,4,128]{3,2,1,0:T(4,128)(2,1)}, bf16[2,2,2,8,2,128,128]{6,5,4,3,2,1,0:T(8,128)(2,1)}, f32[4,8,128]{2,1,0:T(8,128)}, f32[4,8,128]{2,1,0:T(8,128)}) custom-call(bf16[128,8,4,128]{3,2,1,0:T(4,128)(2,1)} %bitcast.48, bf16[128,8,4,128]{3,2,1,0:T(4,128)(2,1)} %bitcast.49, ...), custom_call_target="tpu_custom_call" | custom-call | tf_op jit(solution)/shard_map/inbound/pallas_call | solution.py:184
  73.7 0.9 copy.22
  74.6 0.1 copy.24.delta
  74.7 0.9 copy.21
  75.6 0.1 copy.23.lse
  75.7 0.0 copy-start.2
  75.7 1.2 copy-done.2
  76.9 0.0 copy-start.3
  76.9 1.2 copy-done.3
  78.1 14.1 %grads.1 = (bf16[8,512,128]{2,1,0:T(8,128)(2,1)S(1)}, f32[32,2,128,128]{3,2,1,0:T(8,128)}, bf16[32,2,128,128]{3,2,1,0:T(8,128)(2,1)S(1)}) custom-call(s32[8,5]{1,0:T(8,128)S(1)} %fusion.6.idx, f32[8,5]{1,0:T(8,128)S(1)} %compare_select_fusion.bias, s32[1]{0:T(128)} %bitcast.1.half, f32[8,1,512]{2,1,0:T(1,128)S(1)} %copy.23.lse, ...), custom_call_target="tpu_custom_call" | custom-call | tf_op jit(solution)/shard_map/grads/pallas_call | solution.py:396
  92.2 0.0 copy-start.1
  92.3 2.2 %copy-done.1 = f32[32,2,128,128]{3,2,1,0:T(8,128)S(1)} copy-done((f32[32,2,128,128]{3,2,1,0:T(8,128)S(1)}, f32[32,2,128,128]{3,2,1,0:T(8,128)}, u32[]{:S(2)}) %copy-start.1) | copy-done | bytes 4194328
  94.4 67.5 %outbound.1 = (bf16[128,8,4,128]{3,2,1,0:T(4,128)(2,1)S(1)}, bf16[8,2,128,128]{3,2,1,0:T(8,128)(2,1)S(1)}) custom-call(bf16[8,128,4,128]{3,2,1,0:T(4,128)(2,1)S(1)} %bitcast.42, f32[2,2,8,2,128,128]{5,4,3,2,1,0:T(8,128)S(1)} %bitcast.38, bf16[2,2,8,2,128,128]{5,4,3,2,1,0:T(8,128)(2,1)S(1)} %bitcast.39), custom_call_target="tpu_custom_call" | custom-call | tf_op jit(solution)/shard_map/outbound/pallas_call | solution.py:306
  162.0 0.9 copy.26
  162.9 0.9 copy.25
  163.8 1.0 copy.34
  (2 shorter events, 0.0 us)
Async XLA Ops:
  0.6 0.7 copy-start
  75.7 1.2 copy-start.2
  76.9 1.2 copy-start.3
  92.2 2.2 %copy-start.1 = (f32[32,2,128,128]{3,2,1,0:T(8,128)S(1)}, f32[32,2,128,128]{3,2,1,0:T(8,128)}, u32[]{:S(2)}) copy-start(f32[32,2,128,128]{3,2,1,0:T(8,128)} %get-tuple-element.19) | copy-start | bytes 12582916

commit v3 on v1

v3 whole, which is shorter than its diff:
```python
import functools
import math

import jax
import jax.numpy as jnp
from jax import lax
from jax.experimental import pallas as pl
from jax.experimental.pallas import tpu as pltpu
from jax.sharding import PartitionSpec as P

BLOCK = 128
OFF = -1e30
MESH = pl.DeviceIdType.MESH
NT = (((1,), (1,)), ((), ()))
NN = (((1,), (0,)), ((), ()))
NEAR_FIRST = (0, 1, 7, 2, 6, 3, 5, 4)
WIDE = 4


def near_first(i):
    return jnp.where(i % 2 == 1, (i + 1) // 2, (8 - i // 2) % 8)


class Place:
    def __init__(self, uly, blks, rows):
        self.fold = uly // rows
        self.rows = rows
        self.u, self.slab = lax.axis_index("uly"), lax.axis_index("blk")
        self.y, self.r = self.u // self.fold, self.u % self.fold
        self.z, self.c = self.r // 2, self.r % 2
        self.has_before, self.has_after = self.slab > 0, self.slab < blks - 1
        self.core = self.at(self.z * 2 + 1 - self.c)
        self.other = self.at((1 - self.z) * 2 + self.c)
        self.cross = self.at((1 - self.z) * 2 + 1 - self.c)
        self.after, self.before = {"blk": self.slab + 1}, {"blk": self.slab - 1}
        x = self.slab % WIDE
        inner = self.slab >= WIDE
        self.detours = jnp.logical_and(x == 0, inner)
        self.relays = jnp.logical_and(x == WIDE - 1, inner)
        self.detoured = jnp.logical_and(x == WIDE - 1, self.slab < blks - 1)
        self.relay = {"blk": self.slab + WIDE - 1}
        self.relayed = {"blk": self.slab - WIDE + 1}
        self.relay_to = {"blk": self.slab - WIDE}
        self.relay_from = {"blk": self.slab + WIDE}

    def at(self, r):
        return {"uly": self.y * self.fold + r}

    def row(self, y):
        return {"uly": y * self.fold + self.r}

    def y_at(self, distance):
        return (self.y + distance) % self.rows

    def meet(self):
        barrier = pltpu.get_barrier_semaphore()

        def greet(device):
            pl.semaphore_signal(barrier, inc=1, device_id=device, device_id_type=MESH)

        for d in range(1, self.rows):
            greet(self.row(self.y_at(d)))
        for device in (self.core, self.other, self.cross):
            greet(device)
        count = self.rows + 2
        for there, device in (
            (self.has_after, self.after),
            (self.has_before, self.before),
            (self.detours, self.relay),
            (self.relays, self.relayed),
            (self.relays, self.relay_to),
            (self.detoured, self.relay_from),
        ):
            pl.when(there)(functools.partial(greet, device))
            count = count + there.astype(jnp.int32)
        pl.semaphore_wait(barrier, count)


def remote(src, dst, send, recv, device):
    return pltpu.make_async_remote_copy(
        src_ref=src,
        dst_ref=dst,
        send_sem=send,
        recv_sem=recv,
        device_id=device,
        device_id_type=MESH,
    )


def kernel(uly, blks, scale, idx, bias, slots, q, do, keys, vals, lse, delta,
           grad_q, home, q_parts, do_parts, dq_parts,
           kv, q_all, do_all, lse_all, delta_all, lse_rows, delta_rows, dq_all, terms,
           to_c, from_c, to_x, from_x, relay, to_z, from_z, total, to_y,
           own_s, own_d, part_q, part_do, dq_s, last_s,
           k_ss, k_rs, v_ss, v_rs, q_ss, q_rs, do_ss, do_rs, l_ss, l_rs, e_ss, e_rs,
           z_ss, z_rs, x_ss, x_rs, c_ss, c_rs,
           gq_ss, gq_rs, tc_ss, tc_rs, tx_ss, tx_rs, re_ss, re_rs, fw_ss, tz_ss, tz_rs, ty_ss, ty_rs):
    rows = keys.shape[0]
    group = lse_all.shape[0]
    wide = q_all.shape[1]
    hd = q_all.shape[2]
    select = terms.shape[0] // rows
    me = Place(uly, blks, rows)
    y, r, z, c, slab = me.y, me.r, me.z, me.c, me.slab
    has_after, has_before = me.has_after, me.has_before

    def flat(half, part, zz, t):
        return ((half * 2 + part) * 2 + zz) * rows + t

    def q_part(d):
        t = me.y_at(d)
        return pltpu.make_async_copy(q.at[:, t], q_parts.at[t], part_q.at[d])

    def do_part(d):
        t = me.y_at(d)
        return pltpu.make_async_copy(do.at[:, t], do_parts.at[t], part_do.at[d])

    def rows_of(parts, t):
        return parts.at[t].reshape(wide, hd)

    q_part(0).start()
    do_part(0).start()
    here = kv.at[flat(c, 1, z, y)]
    locals_ = [
        pltpu.make_async_copy(keys.at[y], here.at[0], own_s.at[0]),
        pltpu.make_async_copy(vals.at[y], here.at[1], own_s.at[1]),
        pltpu.make_async_copy(lse.at[slab, :, r], lse_all.at[r], own_s.at[2]),
        pltpu.make_async_copy(delta.at[slab, :, r], delta_all.at[r], own_s.at[3]),
    ]
    for copy in locals_:
        copy.start()
    me.meet()

    sends = []
    for d in NEAR_FIRST[1:]:
        t = me.y_at(d)
        sends.append(remote(keys.at[t], here.at[0], k_ss.at[d], k_rs.at[d], me.row(t)))
        sends.append(remote(vals.at[t], here.at[1], v_ss.at[d], v_rs.at[d], me.row(t)))
    for i in range(1, me.fold):
        t = (r + i) % me.fold
        sends.append(remote(lse.at[slab, :, t], lse_all.at[r], l_ss.at[i], l_rs.at[i], me.at(t)))
        sends.append(
            remote(delta.at[slab, :, t], delta_all.at[r], e_ss.at[i], e_rs.at[i], me.at(t))
        )
    for copy in sends:
        copy.start()
    for d in NEAR_FIRST[1:]:
        t = me.y_at(d)
        sends.append(remote(q.at[:, t], q_parts.at[y], q_ss.at[d], q_rs.at[d], me.row(t)))
        sends[-1].start()
        sends.append(remote(do.at[:, t], do_parts.at[y], do_ss.at[d], do_rs.at[d], me.row(t)))
        sends[-1].start()

    def place(half, part, zz, d):
        return kv.at[flat(half, part, zz, me.y_at(rows - d))]

    def from_row(d):
        there = place(c, 1, z, d)
        remote(there.at[0], there.at[0], k_ss.at[d], k_rs.at[d], me.core).wait_recv()
        remote(there.at[1], there.at[1], v_ss.at[d], v_rs.at[d], me.core).wait_recv()

    def with_other(zz, d):
        there = place(c, 1, zz, d)
        return remote(there, there, z_ss.at[d], z_rs.at[d], me.other)

    def to_after(zz, i, d):
        src, dst = place(c, 1, zz, d), place(c, 0, zz, d)
        return remote(src, dst, x_ss.at[i], x_rs.at[i], me.after)

    def from_before(zz, i, d):
        dst = place(c, 0, zz, d)
        return remote(dst, dst, x_ss.at[i], x_rs.at[i], me.before)

    def with_core(half, part, zz, i, d):
        there = place(half, part, zz, d)
        return remote(there, there, c_ss.at[i], c_rs.at[i], me.core)

    for d in NEAR_FIRST:
        if d == 0:
            locals_[0].wait()
            locals_[1].wait()
        else:
            from_row(d)
        with_other(z, d).start()
        pl.when(has_after)(lambda: to_after(z, d, d).start())
        with_core(c, 1, z, d, d).start()

    locals_[2].wait()
    locals_[3].wait()
    for i in range(1, me.fold):
        t = (r + me.fold - i) % me.fold
        remote(lse_all.at[t], lse_all.at[t], l_ss.at[i], l_rs.at[i], me.core).wait_recv()
        remote(delta_all.at[t], delta_all.at[t], e_ss.at[i], e_rs.at[i], me.core).wait_recv()
    token = lax.broadcasted_iota(jnp.int32, (BLOCK, wide), 0)
    at = lax.broadcasted_iota(jnp.int32, (BLOCK, wide), 1)
    spread = [(at == token * group + s).astype(jnp.float32) for s in range(group)]
    for rows_ref, every in ((lse_rows, lse_all), (delta_rows, delta_all)):
        rows_ref[...] = sum(
            lax.dot_general(
                every[s].reshape(rows, BLOCK),
                spread[s],
                NN,
                precision=lax.Precision.HIGHEST,
                preferred_element_type=jnp.float32,
            )
            for s in range(group)
        )
    terms[rows * select] = jnp.zeros_like(terms[rows * select])

    @pl.loop(0, rows)
    def _(i):
        d = near_first(i)
        with_other(1 - z, d).wait_recv()
        pl.when(has_after)(lambda: to_after(1 - z, rows + d, d).start())
        with_core(c, 1, 1 - z, rows + d, d).start()

        @pl.when(has_before)
        def _():
            from_before(z, d, d).wait_recv()
            with_core(c, 0, z, 2 * rows + d, d).start()

    @pl.when(has_before)
    def _():
        @pl.loop(0, rows)
        def _(i):
            d = near_first(i)
            from_before(1 - z, rows + d, d).wait_recv()
            with_core(c, 0, 1 - z, 3 * rows + d, d).start()

    @pl.when(jnp.logical_not(has_before))
    def _():
        for half in (0, 1):
            first = flat(half, 0, 0, 0)
            for i in range(2 * rows):
                kv[first + i] = jnp.zeros_like(kv[first + i])

    @pl.loop(0, rows)
    def _(d):
        for part, zz, base in ((1, z, 0), (1, 1 - z, rows)):
            with_core(1 - c, part, zz, base + d, d).wait_recv()

        @pl.when(has_before)
        def _():
            for part, zz, base in ((0, z, 2 * rows), (0, 1 - z, 3 * rows)):
                with_core(1 - c, part, zz, base + d, d).wait_recv()

    def dq_part(t, d):
        return pltpu.make_async_copy(dq_all.at[t], rows_of(dq_parts, t), dq_s.at[d])

    def dq_home(t, d):
        return remote(
            dq_parts.at[t], grad_q.at[:, y], gq_ss.at[d], gq_rs.at[d], me.row(t)
        )

    def send_dq(i):
        d = near_first(i)
        t = me.y_at(rows - d)
        dq_part(t, d).wait()

        @pl.when(d == 0)
        def _():
            pltpu.make_async_copy(dq_parts.at[t], grad_q.at[:, t], last_s.at[0]).start()

        pl.when(d > 0)(lambda: dq_home(t, d).start())

    def loads(d):
        t = me.y_at(rows - d)
        return (
            pltpu.make_async_copy(rows_of(q_parts, t), q_all.at[t], part_q.at[d]),
            pltpu.make_async_copy(rows_of(do_parts, t), do_all.at[t], part_do.at[d]),
        )

    q_part(0).wait()
    do_part(0).wait()
    for copy in loads(0):
        copy.start()

    @pl.loop(0, rows)
    def _(i):
        d = near_first(i)
        t = me.y_at(rows - d)

        @pl.when(i < rows - 1)
        def _():
            d = near_first(i + 1)
            t = me.y_at(rows - d)
            remote(q_parts.at[t], q_parts.at[t], q_ss.at[d], q_rs.at[d], me.core).wait_recv()
            remote(do_parts.at[t], do_parts.at[t], do_ss.at[d], do_rs.at[d], me.core).wait_recv()
            for copy in loads(d):
                copy.start()

        for copy in loads(d):
            copy.wait()

        places = [idx[t * select + j] for j in range(select)]
        kcat = jnp.concatenate([kv[p, 0] for p in places], 0)
        vcat = jnp.concatenate([kv[p, 1] for p in places], 0)
        qb, dob = q_all[t], do_all[t]
        s = lax.dot_general(kcat, qb, NT, preferred_element_type=jnp.float32)
        dp = lax.dot_general(vcat, dob, NT, preferred_element_type=jnp.float32)
        lse_row, delta_row = lse_rows[pl.ds(t, 1)], delta_rows[pl.ds(t, 1)]
        probs, dscores = [], []
        for j in range(select):
            part = slice(j * BLOCK, (j + 1) * BLOCK)
            p = jnp.exp(s[part] * scale - (lse_row - bias[t * select + j]))
            if j == 0:
                key_at = lax.broadcasted_iota(jnp.int32, (BLOCK, wide), 0)
                query_at = lax.broadcasted_iota(jnp.int32, (BLOCK, wide), 1) // group
                p = jnp.where(key_at <= query_at, p, 0.0)
            ds = p * (dp[part] - delta_row)
            probs.append(p.astype(jnp.bfloat16))
            dscores.append(ds.astype(jnp.bfloat16))
        pcat = jnp.concatenate(probs, 0)
        dscat = jnp.concatenate(dscores, 0)
        dqt = lax.dot_general(kcat.T, dscat, NN, preferred_element_type=jnp.float32)
        dq_all[t] = (dqt * scale).T.astype(jnp.bfloat16)
        dq_part(t, d).start()
        dk_part = lax.dot_general(dscat, qb, NN, preferred_element_type=jnp.float32) * scale
        dv_part = lax.dot_general(pcat, dob, NN, preferred_element_type=jnp.float32)
        for j in range(select):
            part = slice(j * BLOCK, (j + 1) * BLOCK)
            terms[t * select + j, 0] = dk_part[part]
            terms[t * select + j, 1] = dv_part[part]
        pl.when(i > 0)(lambda: send_dq(i - 1))

    send_dq(rows - 1)

    def gathered(half, part, zz, t):
        at_ = flat(half, part, zz, t) * rows
        x = terms[slots[at_]]
        for b in range(1, rows):
            x = x + terms[slots[at_ + b]]
        return x

    def core(part, zz, order, d):
        t = me.y_at(d)
        i = (part * 2 + order) * rows + d
        place_ = (part * 2 + zz) * rows + t
        return remote(to_c.at[place_], from_c.at[place_], tc_ss.at[i], tc_rs.at[i], me.core)

    def before(zz, order, d):
        t, i = me.y_at(d), order * rows + d
        return remote(to_x.at[zz, t], from_x.at[zz, t], tx_ss.at[i], tx_rs.at[i], me.before)

    def detour(d):
        t = me.y_at(d)
        return remote(to_x.at[z, t], relay.at[t], tx_ss.at[rows + d], re_rs.at[d], me.relay)

    def forward(d):
        t = me.y_at(d)
        return remote(relay.at[t], from_x.at[z, t], fw_ss.at[d], tx_rs.at[rows + d], me.relay_to)

    def relay_in(d):
        t = me.y_at(d)
        return remote(relay.at[t], relay.at[t], re_ss.at[d], re_rs.at[d], me.relayed)

    def other(d):
        t = me.y_at(d)
        return remote(to_z.at[t], from_z.at[t], tz_ss.at[d], tz_rs.at[d], me.other)

    def back(d):
        t = me.y_at(d)
        return remote(to_y.at[t], home.at[y], ty_ss.at[d], ty_rs.at[d], me.row(t))

    direct = jnp.logical_and(has_before, jnp.logical_not(me.detours))
    ways = ((1 - z, 0), (z, 1))
    for part in (0, 1):
        for zz, order in ways:

            @pl.loop(0, rows)
            def _(d):
                t = me.y_at(d)
                to_c[(part * 2 + zz) * rows + t] = gathered(1 - c, part, zz, t).astype(jnp.bfloat16)
                core(part, zz, order, d).start()

    for zz, order in ways:

        @pl.loop(0, rows)
        def _(d):
            t = me.y_at(d)
            core(0, zz, order, d).wait_recv()

            @pl.when(has_before)
            def _():
                x = gathered(c, 0, zz, t) + from_c[zz * rows + t]
                to_x[zz, t] = x.astype(jnp.bfloat16)

            if order == 0:
                pl.when(has_before)(lambda: before(zz, 0, d).start())
            else:
                pl.when(direct)(lambda: before(zz, 1, d).start())
                pl.when(me.detours)(lambda: detour(d).start())

    def summed(zz, order, d, store):
        t = me.y_at(d)
        core(1, zz, order, d).wait_recv()
        x = gathered(c, 1, zz, t) + from_c[(2 + zz) * rows + t]

        @pl.when(has_after)
        def _():
            before(zz, order, d).wait_recv()
            store(t, x + from_x[zz, t])

        pl.when(jnp.logical_not(has_after))(lambda: store(t, x))

    @pl.loop(0, rows)
    def _(d):
        def store(t, x):
            to_z[t] = x.astype(jnp.bfloat16)

        summed(1 - z, 0, d, store)
        other(d).start()

        @pl.when(me.relays)
        def _():
            relay_in(d).wait_recv()
            forward(d).start()

    @pl.loop(0, rows)
    def _(d):
        def store(t, x):
            total[...] = x

        summed(z, 1, d, store)
        other(d).wait_recv()
        t = me.y_at(d)
        to_y[t] = (total[...] + from_z[t]).astype(jnp.bfloat16)
        pl.when(d > 0)(lambda: back(d).start())

    last = pltpu.make_async_copy(to_y.at[y], home.at[y], last_s.at[1])
    last.start()

    for copy in sends:
        copy.wait_send()

    @pl.loop(0, rows)
    def _(d):
        with_other(z, d).wait_send()
        for zz, base in ((z, 0), (1 - z, rows)):
            with_core(c, 1, zz, base + d, d).wait_send()
            pl.when(has_after)(lambda: to_after(zz, base + d, d).wait_send())
            pl.when(has_before)(lambda: with_core(c, 0, zz, 2 * rows + base + d, d).wait_send())
        for part in (0, 1):
            for zz, order in ways:
                core(part, zz, order, d).wait_send()
        for zz, order in ways:
            pl.when(has_before)(lambda: before(zz, order, d).wait_send())
        other(d).wait_send()
        pl.when(me.relays)(lambda: forward(d).wait_send())

    @pl.loop(1, rows)
    def _(d):
        t = me.y_at(rows - d)
        dq_home(t, d).wait_send()
        back(d).wait_send()
        far = me.y_at(d)
        remote(
            dq_parts.at[far], grad_q.at[:, far], gq_ss.at[d], gq_rs.at[d], me.core
        ).wait_recv()
        remote(to_y.at[t], home.at[t], ty_ss.at[d], ty_rs.at[d], me.core).wait_recv()

    pltpu.make_async_copy(dq_parts.at[y], grad_q.at[:, y], last_s.at[0]).wait()
    last.wait()


def shards(queries, keys, values, grad_out, lse, delta, block_keys):
    uly, blks = lax.axis_size("uly"), lax.axis_size("blk")
    tokens, heads, hd = queries.shape
    kvh = keys.shape[1]
    group, fold = heads // kvh, uly // kvh
    wide = tokens * group
    select = block_keys.shape[1]
    u, slab = lax.axis_index("uly"), lax.axis_index("blk")

    own_blocks = lax.dynamic_slice_in_dim(block_keys, slab * uly, uly, 0)
    own_blocks = lax.dynamic_index_in_dim(
        own_blocks.reshape(kvh, fold, -1), u % fold, 1, keepdims=False
    )
    valid = own_blocks >= 0
    own_at = jnp.where(valid, own_blocks, own_blocks[:, :1])
    rel = own_at - (slab - 1) * uly
    part, at = rel // uly, rel % uly
    y, z, c = at // fold, at % fold // 2, at % 2
    idx = ((c * 2 + part) * 2 + z) * kvh + y
    bias = jnp.where(valid, 0.0, OFF).astype(jnp.float32)
    count = kvh * select
    slot = jnp.arange(count, dtype=jnp.int32).reshape(kvh, select)
    listed = (idx == jnp.arange(2 * uly, dtype=jnp.int32)[:, None, None]) & valid
    slots = count + jnp.where(listed, slot - count, 0).sum(2, dtype=jnp.int32)

    low, f32 = jnp.bfloat16, jnp.float32
    hbm, smem = pl.BlockSpec(memory_space=pltpu.HBM), pl.BlockSpec(memory_space=pltpu.SMEM)
    piece = (2, tokens, hd)
    parts = jax.ShapeDtypeStruct((kvh, tokens, group, hd), low)
    dma = pltpu.SemaphoreType.DMA
    by_row = (blks, kvh, fold, 1, tokens)
    grad_q, home, *_ = pl.pallas_call(
        functools.partial(kernel, uly, blks, 1.0 / math.sqrt(hd)),
        out_shape=(
            jax.ShapeDtypeStruct((tokens, kvh, group, hd), low),
            jax.ShapeDtypeStruct((kvh,) + piece, low),
            parts,
            parts,
            parts,
        ),
        in_specs=[smem] * 3 + [hbm] * 6,
        out_specs=(hbm,) * 5,
        scratch_shapes=[
            pltpu.VMEM((2 * uly,) + piece, low),
            pltpu.VMEM((kvh, wide, hd), low),
            pltpu.VMEM((kvh, wide, hd), low),
            pltpu.VMEM((group, kvh, 1, tokens), f32),
            pltpu.VMEM((group, kvh, 1, tokens), f32),
            pltpu.VMEM((kvh, wide), f32),
            pltpu.VMEM((kvh, wide), f32),
            pltpu.VMEM((kvh, wide, hd), low),
            pltpu.VMEM((count + 1,) + piece, f32),
            pltpu.VMEM((uly,) + piece, low),
            pltpu.VMEM((uly,) + piece, low),
            pltpu.VMEM((2, kvh) + piece, low),
            pltpu.VMEM((2, kvh) + piece, low),
            pltpu.VMEM((kvh,) + piece, low),
            pltpu.VMEM((kvh,) + piece, low),
            pltpu.VMEM((kvh,) + piece, low),
            pltpu.VMEM(piece, f32),
            pltpu.VMEM((kvh,) + piece, low),
            dma((6,)),
            dma((6,)),
            dma((kvh,)),
            dma((kvh,)),
            dma((kvh,)),
            dma((2,)),
        ]
        + [dma((kvh,))] * 8
        + [dma((fold,))] * 4
        + [dma((kvh,))] * 2
        + [dma((2 * kvh,))] * 2
        + [dma((4 * kvh,))] * 2
        + [dma((kvh,))] * 2
        + [dma((4 * kvh,))] * 2
        + [dma((2 * kvh,))] * 2
        + [dma((kvh,))] * 7,
        compiler_params=pltpu.CompilerParams(
            collective_id=0, has_side_effects=True, vmem_limit_bytes=56 << 20
        ),
        name="grads",
    )(
        idx.reshape(-1),
        bias.reshape(-1),
        slots.reshape(-1),
        queries.reshape(tokens, kvh, group, hd),
        grad_out.reshape(tokens, kvh, group, hd),
        keys.transpose(1, 0, 2),
        values.transpose(1, 0, 2),
        lse.reshape(by_row),
        delta.reshape(by_row),
    )
    home = home.transpose(1, 2, 0, 3)
    return grad_q.reshape(tokens, heads, hd), home[0], home[1]


def solution(mesh):
    data = P(("blk", "uly"), None, None)
    return jax.shard_map(
        shards,
        mesh=mesh,
        in_specs=(data, data, data, data, P("uly", None), P("uly", None), P()),
        out_specs=(data, data, data),
        check_vma=False,
    )
```

time: 349 us -> 141 us (0.40)
  waiting for transfers between devices: 220 us -> 0 us
  Pallas kernels: 14.3 us -> 131 us
  starting transfers between devices: 68.3 us -> 0 us
  between operations: 14.3 us -> 0.71 us
  other arithmetic: 11.9 us -> 1.4 us
  local copies, waits for them, and re-layouts: 17.4 us -> 8.13 us
    pallas_call x1, Pallas kernels: 14.3 us -> 131 us  [shards(): pl.pallas_call(functools.partial(kernel, uly, blks, 1.0 / math.sqrt(hd)),...]
    all_to_all x11 -> x0, waiting for transfers between devices: 109 us -> none  [over(): lax.all_to_all(x, 'uly', split_axis=0, concat_axis=0, axis_index_groups=g...]
    ppermute x4 -> x0, waiting for transfers between devices: 108 us -> none  [the longest x2 68.4 us: sent_home(): lax.ppermute(acc[:uly].astype(jnp.bfloat16), 'blk', [(i + 1, i) for i in...]
    all_to_all x11 -> x0, starting transfers between devices: 59.3 us -> none  [over(): lax.all_to_all(x, 'uly', split_axis=0, concat_axis=0, axis_index_groups=g...]
    ppermute x4 -> x0, starting transfers between devices: 8.91 us -> none  [the longest x2 4.69 us: sent_home(): lax.ppermute(acc[:uly].astype(jnp.bfloat16), 'blk', [(i + 1, i) for i in...]
    convert_element_type x2 -> x0, other arithmetic: 5.84 us -> none  [sent_home(): total = (acc[uly:] + back).astype(jnp.bfloat16)]
    concatenate x2 -> x0, other arithmetic: 4.18 us -> none  [gathered(): return jnp.concatenate([prev, own], 0)]
    unnamed x18 -> x9, local copies, waits for them, and re-layouts: 6.92 us -> 3.42 us
  transfers between devices with their start and end apart: 17 -> 0, of which waited for: 13 -> 0; matrix products, arithmetic and copies ran while one was open for 7% -> 0% of each run, Pallas kernels for 0% -> 0%
where the time goes in v3:
time: 141 us
  Pallas kernels  131 us (93%)
  local copies, waits for them, and re-layouts  8.13 us (6%)
    pallas_call x1, Pallas kernels, shards(): pl.pallas_call(functools.partial(kernel, uly, blks, 1.0 / math.sqrt(hd)),...  131 us
    unnamed x9, local copies, waits for them, and re-layouts  3.42 us

profile of v3, /device:TPU:6, one launch (start us, length us, event | category | flops | bytes accessed | tf_op | source)
XLA Modules:
  0.0 141.0 jit_solution(7991840781246852379)
XLA Ops:
  0.6 0.0 copy-start
  0.6 0.0 copy-start.2
  0.7 0.7 copy-done
  1.4 0.1 constant_dynamic-slice_fusion.1
  1.4 0.1 copy.24
  1.5 0.1 reshape.148
  1.6 0.1 constant_dynamic-slice_fusion
  1.7 0.1 copy.20
  1.8 0.1 slice_reduce_fusion
  1.9 0.1 squeeze.12
  2.0 0.6 compare_select_fusion.bias
  2.6 0.1 fusion.6
  2.7 0.1 copy.22
  2.8 0.1 copy.23
  2.9 0.1 select_reduce_fusion
  3.0 0.1 broadcast_in_dim.32
  3.0 0.1 broadcast_in_dim.33
  3.1 0.6 multiply_add_fusion.idx
  3.7 0.1 copy.25
  3.8 0.7 add.124.slots
  4.5 0.0 copy-done.2
  4.5 1.8 %copy_bitcast_fusion = (bf16[8,128,128]{2,1,0:T(8,128)(2,1)}, bf16[8,128,128]{2,1,0:T(8,128)(2,1)}) fusion(bf16[128,8,128]{2,1,0:T(8,128)(2,1)S(1)} %copy-done.2, bf16[128,8,128]{2,1,0:T(8,128)(2,1)} %param.8), kind=kLoop, calls=%fused_computation.2 | loop fusion | bytes 1048576 | tf_op jit(solution)/shard_map/transpose | solution.py:554
  6.3 130.8 %grads.1 = (bf16[128,8,4,128]{3,2,1,0:T(4,128)(2,1)}, bf16[8,2,128,128]{3,2,1,0:T(8,128)(2,1)}, bf16[8,128,4,128]{3,2,1,0:T(4,128)(2,1)}, bf16[8,128,4,128]{3,2,1,0:T(4,128)(2,1)}, bf16[8,128,4,128]{3,2,1,0:T(4,128)(2,1)}) custom-call(s32[40]{0:T(128)} %multiply_add_fusion.idx, f32[40]{0:T(128)} %compare_select_fusion.bias, s32[512]{0:T(512)} %add.124.slots, ...), custom_call_target="tpu_custom_call" | custom-call | tf_op jit(solution)/shard_map/grads/pallas_call | solution.py:497
  137.1 0.0 copy-start.1
  137.1 1.2 slice_bitcast_fusion
  138.3 0.9 copy.29
  139.2 0.9 copy.28
  140.0 0.0 copy-done.1
  140.0 1.0 copy.33
  (3 shorter events, 0.0 us)
Async XLA Ops:
  0.6 0.7 copy-start
  0.6 3.9 %copy-start.2 = (bf16[128,8,128]{2,1,0:T(8,128)(2,1)S(1)}, bf16[128,8,128]{2,1,0:T(8,128)(2,1)}, u32[]{:S(2)}) copy-start(bf16[128,8,128]{2,1,0:T(8,128)(2,1)} %param.9) | copy-start | bytes 786436
  137.1 2.9 %copy-start.1 = (bf16[128,8,4,128]{3,2,1,0:T(4,128)(2,1)S(1)}, bf16[128,8,4,128]{3,2,1,0:T(4,128)(2,1)}, u32[]{:S(2)}) copy-start(bf16[128,8,4,128]{3,2,1,0:T(4,128)(2,1)} %get-tuple-element.5) | copy-start | bytes 3145732

commit v4 on v3

--- a/solution.py
+++ b/solution.py
@@ -33,15 +33,16 @@
         self.other = self.at((1 - self.z) * 2 + self.c)
         self.cross = self.at((1 - self.z) * 2 + 1 - self.c)
         self.after, self.before = {"blk": self.slab + 1}, {"blk": self.slab - 1}
-        x = self.slab % WIDE
-        inner = self.slab >= WIDE
-        self.detours = jnp.logical_and(x == 0, inner)
-        self.relays = jnp.logical_and(x == WIDE - 1, inner)
-        self.detoured = jnp.logical_and(x == WIDE - 1, self.slab < blks - 1)
-        self.relay = {"blk": self.slab + WIDE - 1}
-        self.relayed = {"blk": self.slab - WIDE + 1}
-        self.relay_to = {"blk": self.slab - WIDE}
-        self.relay_from = {"blk": self.slab + WIDE}
+        self.x = self.slab % WIDE
+        run, runs = self.slab // WIDE, blks // WIDE
+        self.ends = jnp.logical_and(self.x == WIDE - 1, run < runs - 1)
+        self.starts = jnp.logical_and(self.x == 0, run > 0)
+        self.carries = jnp.logical_and(self.x < WIDE - 1, run < runs - 1)
+        self.returns = jnp.logical_and(self.x > 0, run > 0)
+        self.blks = blks
+
+    def column(self, x):
+        return {"blk": self.slab - self.x + x}
 
     def at(self, r):
         return {"uly": self.y * self.fold + r}
@@ -63,16 +64,13 @@
         for device in (self.core, self.other, self.cross):
             greet(device)
         count = self.rows + 2
-        for there, device in (
-            (self.has_after, self.after),
-            (self.has_before, self.before),
-            (self.detours, self.relay),
-            (self.relays, self.relayed),
-            (self.relays, self.relay_to),
-            (self.detoured, self.relay_from),
-        ):
-            pl.when(there)(functools.partial(greet, device))
-            count = count + there.astype(jnp.int32)
+        for k in range(1, WIDE + 1):
+            for there, device in (
+                (self.slab + k < self.blks, {"blk": self.slab + k}),
+                (self.slab >= k, {"blk": self.slab - k}),
+            ):
+                pl.when(there)(functools.partial(greet, device))
+                count = count + there.astype(jnp.int32)
         pl.semaphore_wait(barrier, count)
 
 
@@ -88,13 +86,13 @@
 
 
 def kernel(uly, blks, scale, idx, bias, slots, q, do, keys, vals, lse, delta,
-           grad_q, home, q_parts, do_parts, dq_parts,
+           grad_q, home_k, home_v, q_parts, do_parts, dq_parts,
            kv, q_all, do_all, lse_all, delta_all, lse_rows, delta_rows, dq_all, terms,
-           to_c, from_c, to_x, from_x, relay, to_z, from_z, total, to_y,
+           to_c, from_c, to_x, from_x, carried, relay, to_z, from_z, total, to_y,
            own_s, own_d, part_q, part_do, dq_s, last_s,
            k_ss, k_rs, v_ss, v_rs, q_ss, q_rs, do_ss, do_rs, l_ss, l_rs, e_ss, e_rs,
            z_ss, z_rs, x_ss, x_rs, c_ss, c_rs,
-           gq_ss, gq_rs, tc_ss, tc_rs, tx_ss, tx_rs, re_ss, re_rs, fw_ss, tz_ss, tz_rs, ty_ss, ty_rs):
+           gq_ss, gq_rs, tc_ss, tc_rs, tx_ss, tx_rs, re_ss, re_rs, fw_ss, tz_ss, tz_rs, ty_ss, ty_rs, tv_ss, tv_rs, ca_rs, cf_ss):
     rows = keys.shape[0]
     group = lse_all.shape[0]
     wide = q_all.shape[1]
@@ -144,12 +142,18 @@
         )
     for copy in sends:
         copy.start()
-    for d in NEAR_FIRST[1:]:
-        t = me.y_at(d)
-        sends.append(remote(q.at[:, t], q_parts.at[y], q_ss.at[d], q_rs.at[d], me.row(t)))
-        sends[-1].start()
-        sends.append(remote(do.at[:, t], do_parts.at[y], do_ss.at[d], do_rs.at[d], me.row(t)))
-        sends[-1].start()
+
+    def send_queries(distances):
+        for d in distances:
+            t = me.y_at(d)
+            for copy in (
+                remote(q.at[:, t], q_parts.at[y], q_ss.at[d], q_rs.at[d], me.row(t)),
+                remote(do.at[:, t], do_parts.at[y], do_ss.at[d], do_rs.at[d], me.row(t)),
+            ):
+                copy.start()
+                sends.append(copy)
+
+    send_queries((1, 7, 2))
 
     def place(half, part, zz, d):
         return kv.at[flat(half, part, zz, me.y_at(rows - d))]
@@ -166,6 +170,36 @@
     def to_after(zz, i, d):
         src, dst = place(c, 1, zz, d), place(c, 0, zz, d)
         return remote(src, dst, x_ss.at[i], x_rs.at[i], me.after)
+
+    def pass_on(zz, order, d):
+        i = order * rows + d
+        straight = jnp.logical_or(jnp.logical_not(me.ends), d % WIDE == WIDE - 1)
+        pl.when(jnp.logical_and(has_after, straight))(lambda: to_after(zz, i, d).start())
+
+        @pl.when(jnp.logical_not(straight))
+        def _():
+            k = order * 2 + d // WIDE
+            remote(
+                place(c, 1, zz, d), carried.at[k], x_ss.at[i], ca_rs.at[k], me.column(d % WIDE)
+            ).start()
+
+    def carry(zz, order, k):
+        d = me.x + k * WIDE
+        at_ = order * 2 + k
+        dst = place(c, 0, zz, d)
+        return remote(
+            carried.at[at_], dst, cf_ss.at[at_], x_rs.at[order * rows + d], me.column(WIDE)
+        )
+
+    def carry_on(zz, order):
+        @pl.when(me.carries)
+        def _():
+            for k in (0, 1):
+                at_ = order * 2 + k
+                remote(
+                    carried.at[at_], carried.at[at_], cf_ss.at[at_], ca_rs.at[at_], me.core
+                ).wait_recv()
+                carry(zz, order, k).start()
 
     def from_before(zz, i, d):
         dst = place(c, 0, zz, d)
@@ -182,8 +216,11 @@
         else:
             from_row(d)
         with_other(z, d).start()
-        pl.when(has_after)(lambda: to_after(z, d, d).start())
+        pass_on(z, 0, jnp.int32(d))
         with_core(c, 1, z, d, d).start()
+
+    send_queries((6, 3))
+    carry_on(z, 0)
 
     locals_[2].wait()
     locals_[3].wait()
@@ -207,17 +244,21 @@
         )
     terms[rows * select] = jnp.zeros_like(terms[rows * select])
 
-    @pl.loop(0, rows)
-    def _(i):
+    def hand_on(i):
         d = near_first(i)
         with_other(1 - z, d).wait_recv()
-        pl.when(has_after)(lambda: to_after(1 - z, rows + d, d).start())
+        pass_on(1 - z, 1, d)
         with_core(c, 1, 1 - z, rows + d, d).start()
 
         @pl.when(has_before)
         def _():
             from_before(z, d, d).wait_recv()
             with_core(c, 0, z, 2 * rows + d, d).start()
+
+    pl.loop(0, rows // 2)(hand_on)
+    send_queries((5, 4))
+    pl.loop(rows // 2, rows)(hand_on)
+    carry_on(1 - z, 1)
 
     @pl.when(has_before)
     def _():
@@ -342,17 +383,25 @@
         t, i = me.y_at(d), order * rows + d
         return remote(to_x.at[zz, t], from_x.at[zz, t], tx_ss.at[i], tx_rs.at[i], me.before)
 
-    def detour(d):
-        t = me.y_at(d)
-        return remote(to_x.at[z, t], relay.at[t], tx_ss.at[rows + d], re_rs.at[d], me.relay)
-
-    def forward(d):
-        t = me.y_at(d)
-        return remote(relay.at[t], from_x.at[z, t], fw_ss.at[d], tx_rs.at[rows + d], me.relay_to)
-
-    def relay_in(d):
-        t = me.y_at(d)
-        return remote(relay.at[t], relay.at[t], re_ss.at[d], re_rs.at[d], me.relayed)
+    def detour(zz, order, d):
+        t, k = me.y_at(d), order * 2 + d // WIDE
+        return remote(
+            to_x.at[zz, t], relay.at[k], tx_ss.at[order * rows + d], re_rs.at[k], me.column(d % WIDE)
+        )
+
+    def forward(zz, order, k):
+        d = me.x + k * WIDE
+        at_ = order * 2 + k
+        return remote(
+            relay.at[at_],
+            from_x.at[zz, me.y_at(d)],
+            fw_ss.at[at_],
+            tx_rs.at[order * rows + d],
+            me.column(-1),
+        )
+
+    def relay_in(k):
+        return remote(relay.at[k], relay.at[k], re_ss.at[k], re_rs.at[k], me.core)
 
     def other(d):
         t = me.y_at(d)
@@ -360,36 +409,82 @@
 
     def back(d):
         t = me.y_at(d)
-        return remote(to_y.at[t], home.at[y], ty_ss.at[d], ty_rs.at[d], me.row(t))
-
-    direct = jnp.logical_and(has_before, jnp.logical_not(me.detours))
+        return (
+            remote(to_y.at[t, 0], home_k.at[y], ty_ss.at[d], ty_rs.at[d], me.row(t)),
+            remote(to_y.at[t, 1], home_v.at[y], tv_ss.at[d], tv_rs.at[d], me.row(t)),
+        )
+
+    def start_back(d):
+        for copy in back(d):
+            copy.start()
+
+    direct = jnp.logical_and(has_before, jnp.logical_not(me.starts))
+
+    def offer(part, zz, order, d):
+        t = me.y_at(d)
+        to_c[(part * 2 + zz) * rows + t] = gathered(1 - c, part, zz, t).astype(jnp.bfloat16)
+        core(part, zz, order, d).start()
+
+    def collect(zz, order, d):
+        t = me.y_at(d)
+        core(0, zz, order, d).wait_recv()
+        x = gathered(c, 0, zz, t) + from_c[zz * rows + t]
+        to_x[zz, t] = x.astype(jnp.bfloat16)
+
     ways = ((1 - z, 0), (z, 1))
-    for part in (0, 1):
+
+    @pl.loop(0, rows)
+    def _(d):
+        offer(0, 1 - z, 0, d)
+
+        @pl.when(jnp.logical_not(direct))
+        def _():
+            offer(0, z, 1, d)
+
+    @pl.loop(0, rows)
+    def _(d):
+        @pl.when(has_before)
+        def _():
+            collect(1 - z, 0, d)
+
+        straight = jnp.logical_or(direct, jnp.logical_and(me.starts, d % WIDE == 0))
+        pl.when(straight)(lambda: before(1 - z, 0, d).start())
+
+        @pl.when(me.starts)
+        def _():
+            pl.when(d % WIDE > 0)(lambda: detour(1 - z, 0, d).start())
+            collect(z, 1, d)
+            pl.when(d % WIDE == 0)(lambda: before(z, 1, d).start())
+            pl.when(d % WIDE > 0)(lambda: detour(z, 1, d).start())
+
+    @pl.when(me.returns)
+    def _():
         for zz, order in ways:
-
-            @pl.loop(0, rows)
-            def _(d):
-                t = me.y_at(d)
-                to_c[(part * 2 + zz) * rows + t] = gathered(1 - c, part, zz, t).astype(jnp.bfloat16)
-                core(part, zz, order, d).start()
-
-    for zz, order in ways:
-
+            for k in (0, 1):
+                relay_in(order * 2 + k).wait_recv()
+                forward(zz, order, k).start()
+
+    @pl.when(direct)
+    def _():
         @pl.loop(0, rows)
         def _(d):
-            t = me.y_at(d)
-            core(0, zz, order, d).wait_recv()
-
-            @pl.when(has_before)
-            def _():
-                x = gathered(c, 0, zz, t) + from_c[zz * rows + t]
-                to_x[zz, t] = x.astype(jnp.bfloat16)
-
-            if order == 0:
-                pl.when(has_before)(lambda: before(zz, 0, d).start())
-            else:
-                pl.when(direct)(lambda: before(zz, 1, d).start())
-                pl.when(me.detours)(lambda: detour(d).start())
+            offer(0, z, 1, d)
+
+    @pl.loop(0, rows)
+    def _(d):
+        @pl.when(direct)
+        def _():
+            collect(z, 1, d)
+            before(z, 1, d).start()
+
+        offer(1, 1 - z, 0, d)
+
+    @pl.when(jnp.logical_not(has_before))
+    def _():
+        @pl.loop(0, rows)
+        def _(d):
+            core(0, 1 - z, 0, d).wait_recv()
+            core(0, z, 1, d).wait_recv()
 
     def summed(zz, order, d, store):
         t = me.y_at(d)
@@ -408,14 +503,10 @@
         def store(t, x):
             to_z[t] = x.astype(jnp.bfloat16)
 
+        offer(1, z, 1, d)
         summed(1 - z, 0, d, store)
         other(d).start()
 
-        @pl.when(me.relays)
-        def _():
-            relay_in(d).wait_recv()
-            forward(d).start()
-
     @pl.loop(0, rows)
     def _(d):
         def store(t, x):
@@ -425,10 +516,14 @@
         other(d).wait_recv()
         t = me.y_at(d)
         to_y[t] = (total[...] + from_z[t]).astype(jnp.bfloat16)
-        pl.when(d > 0)(lambda: back(d).start())
-
-    last = pltpu.make_async_copy(to_y.at[y], home.at[y], last_s.at[1])
-    last.start()
+        pl.when(d > 0)(lambda: start_back(d))
+
+    last = (
+        pltpu.make_async_copy(to_y.at[y, 0], home_k.at[y], last_s.at[1]),
+        pltpu.make_async_copy(to_y.at[y, 1], home_v.at[y], last_s.at[2]),
+    )
+    for copy in last:
+        copy.start()
 
     for copy in sends:
         copy.wait_send()
@@ -446,21 +541,28 @@
         for zz, order in ways:
             pl.when(has_before)(lambda: before(zz, order, d).wait_send())
         other(d).wait_send()
-        pl.when(me.relays)(lambda: forward(d).wait_send())
+
+    for k in (0, 1):
+        for order, zz in ((0, z), (1, 1 - z)):
+            pl.when(me.carries)(lambda: carry(zz, order, k).wait_send())
+            pl.when(me.returns)(lambda: forward(zz, order, k).wait_send())
 
     @pl.loop(1, rows)
     def _(d):
         t = me.y_at(rows - d)
         dq_home(t, d).wait_send()
-        back(d).wait_send()
+        for copy in back(d):
+            copy.wait_send()
         far = me.y_at(d)
         remote(
             dq_parts.at[far], grad_q.at[:, far], gq_ss.at[d], gq_rs.at[d], me.core
         ).wait_recv()
-        remote(to_y.at[t], home.at[t], ty_ss.at[d], ty_rs.at[d], me.core).wait_recv()
+        remote(home_k.at[t], home_k.at[t], ty_ss.at[d], ty_rs.at[d], me.core).wait_recv()
+        remote(home_v.at[t], home_v.at[t], tv_ss.at[d], tv_rs.at[d], me.core).wait_recv()
 
     pltpu.make_async_copy(dq_parts.at[y], grad_q.at[:, y], last_s.at[0]).wait()
-    last.wait()
+    for copy in last:
+        copy.wait()
 
 
 def shards(queries, keys, values, grad_out, lse, delta, block_keys):
@@ -494,17 +596,18 @@
     parts = jax.ShapeDtypeStruct((kvh, tokens, group, hd), low)
     dma = pltpu.SemaphoreType.DMA
     by_row = (blks, kvh, fold, 1, tokens)
-    grad_q, home, *_ = pl.pallas_call(
+    grad_q, home_k, home_v, *_ = pl.pallas_call(
         functools.partial(kernel, uly, blks, 1.0 / math.sqrt(hd)),
         out_shape=(
             jax.ShapeDtypeStruct((tokens, kvh, group, hd), low),
-            jax.ShapeDtypeStruct((kvh,) + piece, low),
+            jax.ShapeDtypeStruct((kvh,) + piece[1:], low),
+            jax.ShapeDtypeStruct((kvh,) + piece[1:], low),
             parts,
             parts,
             parts,
         ),
         in_specs=[smem] * 3 + [hbm] * 6,
-        out_specs=(hbm,) * 5,
+        out_specs=(hbm,) * 6,
         scratch_shapes=[
             pltpu.VMEM((2 * uly,) + piece, low),
             pltpu.VMEM((kvh, wide, hd), low),
@@ -519,7 +622,8 @@
             pltpu.VMEM((uly,) + piece, low),
             pltpu.VMEM((2, kvh) + piece, low),
             pltpu.VMEM((2, kvh) + piece, low),
-            pltpu.VMEM((kvh,) + piece, low),
+            pltpu.VMEM((4,) + piece, low),
+            pltpu.VMEM((4,) + piece, low),
             pltpu.VMEM((kvh,) + piece, low),
             pltpu.VMEM((kvh,) + piece, low),
             pltpu.VMEM(piece, f32),
@@ -529,7 +633,7 @@
             dma((kvh,)),
             dma((kvh,)),
             dma((kvh,)),
-            dma((2,)),
+            dma((3,)),
         ]
         + [dma((kvh,))] * 8
         + [dma((fold,))] * 4
@@ -539,7 +643,7 @@
         + [dma((kvh,))] * 2
         + [dma((4 * kvh,))] * 2
         + [dma((2 * kvh,))] * 2
-        + [dma((kvh,))] * 7,
+        + [dma((kvh,))] * 11,
         compiler_params=pltpu.CompilerParams(
             collective_id=0, has_side_effects=True, vmem_limit_bytes=56 << 20
         ),
@@ -555,8 +659,11 @@
         lse.reshape(by_row),
         delta.reshape(by_row),
     )
-    home = home.transpose(1, 2, 0, 3)
-    return grad_q.reshape(tokens, heads, hd), home[0], home[1]
+    return (
+        grad_q.reshape(tokens, heads, hd),
+        home_k.transpose(1, 0, 2),
+        home_v.transpose(1, 0, 2),
+    )
 
 
 def solution(mesh):

time: 141 us -> 142 us (level)
  the two profiles are of different devices: /device:TPU:6 before, /device:TPU:79 now
where the time goes in v4:
time: 142 us
  Pallas kernels  131 us (92%)
  local copies, waits for them, and re-layouts  8.96 us (6%)
    pallas_call x1, Pallas kernels, shards(): pl.pallas_call(functools.partial(kernel, uly, blks, 1.0 / math.sqrt(hd)),...  131 us
    unnamed x9, local copies, waits for them, and re-layouts  5.4 us

profile of v4, /device:TPU:79, one launch (start us, length us, event | category | flops | bytes accessed | tf_op | source)
XLA Modules:
  0.0 142.1 jit_solution(11391625446688911001)
XLA Ops:
  0.6 0.0 copy-start
  0.6 0.0 copy-start.2
  0.7 0.7 copy-done
  1.4 0.1 constant_dynamic-slice_fusion.1
  1.4 0.1 copy.24
  1.5 0.1 reshape.148
  1.6 0.1 constant_dynamic-slice_fusion
  1.7 0.1 copy.20
  1.8 0.1 slice_reduce_fusion
  1.9 0.1 squeeze.6
  2.0 0.6 compare_select_fusion.bias
  2.6 0.1 fusion.6
  2.7 0.1 copy.22
  2.8 0.1 copy.23
  2.9 0.1 select_reduce_fusion
  3.0 0.1 broadcast_in_dim.32
  3.1 0.1 broadcast_in_dim.33
  3.1 0.5 multiply_add_fusion.idx
  3.7 0.1 copy.25
  3.7 0.7 add.124.slots
  4.4 0.0 copy-done.2
  4.4 1.8 %copy_bitcast_fusion = (bf16[8,128,128]{2,1,0:T(8,128)(2,1)}, bf16[8,128,128]{2,1,0:T(8,128)(2,1)}) fusion(bf16[128,8,128]{2,1,0:T(8,128)(2,1)S(1)} %copy-done.2, bf16[128,8,128]{2,1,0:T(8,128)(2,1)} %param.8), kind=kLoop, calls=%fused_computation | loop fusion | bytes 1048576 | tf_op jit(solution)/shard_map/transpose | solution.py:658
  6.2 131.1 %grads.1 = (bf16[128,8,4,128]{3,2,1,0:T(4,128)(2,1)}, bf16[8,128,128]{2,1,0:T(8,128)(2,1)}, bf16[8,128,128]{2,1,0:T(8,128)(2,1)}, bf16[8,128,4,128]{3,2,1,0:T(4,...) custom-call(s32[40]{0:T(128)} %multiply_add_fusion.idx, f32[40]{0:T(128)} %compare_select_fusion.bias, ...), custom_call_target="tpu_custom_call" | custom-call | tf_op jit(solution)/shard_map/grads/pallas_call | solution.py:599
  137.3 0.0 copy-start.1
  137.4 1.9 %copy.28 = bf16[128,8,128]{2,1,0:T(8,128)(2,1)} copy(bf16[128,8,128]{2,0,1:T(8,128)(2,1)} %bitcast.24) | data formatting | bytes 524288
  139.3 1.8 %copy.29 = bf16[128,8,128]{2,1,0:T(8,128)(2,1)} copy(bf16[128,8,128]{2,0,1:T(8,128)(2,1)} %bitcast.23) | data formatting | bytes 524288
  141.1 0.0 copy-done.1
  141.1 1.0 copy.33
  (3 shorter events, 0.0 us)
Async XLA Ops:
  0.6 0.7 copy-start
  0.6 3.8 %copy-start.2 = (bf16[128,8,128]{2,1,0:T(8,128)(2,1)S(1)}, bf16[128,8,128]{2,1,0:T(8,128)(2,1)}, u32[]{:S(2)}) copy-start(bf16[128,8,128]{2,1,0:T(8,128)(2,1)} %param.9) | copy-start | bytes 786436
  137.3 3.8 %copy-start.1 = (bf16[128,8,4,128]{3,2,1,0:T(4,128)(2,1)S(1)}, bf16[128,8,4,128]{3,2,1,0:T(4,128)(2,1)}, u32[]{:S(2)}) copy-start(bf16[128,8,4,128]{3,2,1,0:T(4,128)(2,1)} %get-tuple-element.6) | copy-start | bytes 3145732
